TPU v7x, 32 devices: a whole 2x2x4 slice. The times are simulated.
32 devices in a mesh: dp: 8 (over z, y), row: 2 (over x), col: 2 (over core).
Axes of the slice: x: 2, y: 2, z: 4, core: 2. Of those that a mesh axis runs over, the one named last changes fastest.
Arguments:
- hidden: bfloat16 [6144, 1024], P('dp'), may hold values from -26 to 26
- out_grad: bfloat16 [6144, 1024], P('dp', 'row'), may hold values from -4 to 4
- seq_lens: int32 [8, 4], P('dp'), may hold values from 1 to 765, as said below
- rmsnorm_gain: float32 [1024], P('row'), may hold values from 0.5 to 1.5
- w_z: bfloat16 [1024, 2048], P('row', 'col'), may hold values from -0.1875 to 0.1875
- w_x: bfloat16 [1024, 2048], P('row', 'col'), may hold values from -0.1875 to 0.1875
- w_bc: bfloat16 [1024, 256], P('row', 'col'), may hold values from -0.1875 to 0.1875
- w_dt: bfloat16 [1024, 32], P('row', 'col'), may hold values from -0.1875 to 0.1875
- conv_x: float32 [4, 2, 1024], P(None, 'col', 'row'), may hold values from -3 to 3
- conv_x_bias: float32 [2, 1024], P('col', 'row'), may hold values from -3 to 3
- conv_bc: float32 [4, 256], replicated, may hold values from -3 to 3
- conv_bc_bias: float32 [256], replicated, may hold values from -3 to 3
- dt_bias: float32 [2, 16], P('col', 'row'), may hold values from -7.5 to -4.5
- a_log: float32 [2, 16], P('col', 'row'), may hold values from 0 to 2.1
- d_skip: float32 [2, 16], P('col', 'row'), may hold values from 0.3 to 3
- gate_gain: float32 [2, 1024], P('col', 'row'), may hold values from 0.5 to 1.5
- w_out: bfloat16 [2048, 1024], P('col', 'row'), may hold values from -0.125 to 0.125
Outputs:
- block_out: bfloat16 [6144, 1024], P('dp', ('row', 'col'))
- hidden_input_gradient: bfloat16 [6144, 1024], P('dp', ('row', 'col'))
- grad_norm_gain: float32 [1024], P(('row', 'col'))
- grad_w_z: float32 [1024, 2048], P('row', 'col')
- grad_w_x: float32 [1024, 2048], P('row', 'col')
- grad_w_bc: float32 [1024, 256], P('row', 'col')
- grad_w_dt: float32 [1024, 32], P('row', 'col')
- grad_conv_x: float32 [4, 2, 1024], P(None, 'col', 'row')
- grad_conv_x_bias: float32 [2, 1024], P('col', 'row')
- grad_conv_bc: float32 [4, 256], replicated
- grad_conv_bc_bias: float32 [256], replicated
- grad_dt_bias: float32 [2, 16], P('col', 'row')
- grad_a_log: float32 [2, 16], P('col', 'row')
- grad_d_skip: float32 [2, 16], P('col', 'row')
- grad_gate_gain: float32 [2, 1024], P('col', 'row')
- grad_w_out: float32 [2048, 1024], P('col', 'row')
Inputs may be any that keep to these rules, and one draw needn't show every extreme that they name: `seq_lens`: row d lists the lengths of the 4 sequences of index d of dp in the order in which they lie in its 768 token rows from row 0; each row sums to at most 768, some row to exactly 768 with one sequence of the largest length, and the rows after a row's sequences are padding.
All inputs are finite; a program needn't handle non-finite values.
Results may differ from a plain program's by a relative error of at most 0.0078.
Values may be sent and summed in bfloat16 or wider, within the bound.
A program may use at most 192 MiB of HBM per device.

v0:
```python
import jax
import jax.numpy as jnp
from jax import lax
from jax.sharding import PartitionSpec as P

MODEL_WIDTH = 1024
E = 2048


EPS = 1e-05
HIGHEST = lax.Precision.HIGHEST


def segments(lengths, row_count):
    ends = jnp.cumsum(lengths)
    places = jnp.arange(row_count, dtype=jnp.int32)
    segment = jnp.sum((places[:, None] >= ends[None, :]).astype(jnp.int32), axis=1)
    living = (segment < lengths.shape[0]).astype(jnp.float32)
    return (segment, living)


def depthwise(signal, weights, offset_bias, segment):
    row_count = signal.shape[0]
    total = offset_bias[None, :] + weights[0][None, :] * signal
    for offset in range(1, weights.shape[0]):
        moved = jnp.concatenate(
            [jnp.zeros((offset, signal.shape[1]), jnp.float32), signal[: row_count - offset]],
            axis=0,
        )
        earlier = jnp.concatenate(
            [jnp.full((offset,), -1, jnp.int32), segment[: row_count - offset]]
        )
        same_seq = (earlier == segment).astype(jnp.float32)
        total = total + weights[offset][None, :] * moved * same_seq[:, None]
    return total


def state_scan(inputs, b_rows, c_rows, steps, rates, segment, block):
    row_count, heads, head_width = inputs.shape
    width_state = b_rows.shape[1]
    count = row_count // block
    series = (
        inputs.reshape(count, block, heads, head_width),
        b_rows.reshape(count, block, width_state),
        c_rows.reshape(count, block, width_state),
        steps.reshape(count, block, heads),
        segment.reshape(count, block),
    )
    places = jnp.arange(block, dtype=jnp.int32)
    causal = places[:, None] >= places[None, :]

    def advance(carry, pieces):
        state, previous = carry
        x_blk, b_blk, c_blk, step_blk, seg_blk = pieces
        logs = jnp.cumsum(-step_blk * rates[None, :], axis=0)
        same = jnp.logical_and(seg_blk[:, None] == seg_blk[None, :], causal)
        gaps = logs.T[:, :, None] - logs.T[:, None, :]
        decays = jnp.where(same[None], jnp.exp(jnp.where(same[None], gaps, 0.0)), 0.0)
        scores = jnp.dot(c_blk, b_blk.T, precision=HIGHEST)
        weighted = x_blk * step_blk[:, :, None]
        inner = jnp.einsum("hts,shp->thp", decays * scores[None], weighted, precision=HIGHEST)
        keeps = (seg_blk == previous).astype(jnp.float32)
        carried = jnp.einsum("tn,hpn->thp", c_blk, state, precision=HIGHEST)
        carried = carried * (jnp.exp(logs) * keeps[:, None])[:, :, None]
        closing = (
            jnp.exp(logs[-1][None, :] - logs)
            * (seg_blk == seg_blk[-1]).astype(jnp.float32)[:, None]
        )
        fresh = jnp.einsum("shp,sn->hpn", weighted * closing[:, :, None], b_blk, precision=HIGHEST)
        held = jnp.exp(logs[-1]) * (seg_blk[-1] == previous).astype(jnp.float32)
        state = state * held[:, None, None] + fresh
        return ((state, seg_blk[-1]), inner + carried)

    start = (jnp.zeros((heads, head_width, width_state), jnp.float32), jnp.array(-1, jnp.int32))
    final_carry, outputs = lax.scan(advance, start, series)
    return outputs.reshape(row_count, heads, head_width)


def mixer(
    x_part,
    bc_part,
    z_part,
    dt_part,
    conv_w,
    conv_b,
    bc_w,
    bc_b,
    dt_shift,
    a_logs,
    skips,
    segment,
    living,
):
    row_count = x_part.shape[0]
    heads = dt_shift.shape[0]
    x_act = jax.nn.silu(depthwise(x_part, conv_w, conv_b, segment))
    bc_act = jax.nn.silu(depthwise(bc_part, bc_w, bc_b, segment))
    width_state = bc_act.shape[1] // 2
    steps = jax.nn.softplus(dt_part + dt_shift[None, :])
    inputs = x_act.reshape(row_count, heads, -1)
    block = min(row_count, 256)
    scanned = state_scan(
        inputs,
        bc_act[:, :width_state],
        bc_act[:, width_state:],
        steps,
        jnp.exp(a_logs),
        segment,
        block,
    )
    scanned = scanned + skips[None, :, None] * inputs
    return scanned.reshape(row_count, -1) * jax.nn.silu(z_part) * living[:, None]


def per_device(
    hidden,
    out_grad,
    seq_lens,
    rmsnorm_gain,
    w_z,
    w_x,
    w_bc,
    w_dt,
    conv_x,
    conv_x_bias,
    conv_bc,
    conv_bc_bias,
    dt_bias,
    a_log,
    d_skip,
    gate_gain,
    w_out,
):
    row_count = hidden.shape[0]
    width_of_row = w_z.shape[0]
    fourth_share = width_of_row // lax.axis_size("col")
    index_of_row = lax.axis_index("row")
    col_index = lax.axis_index("col")
    local_begin = (index_of_row * lax.axis_size("col") + col_index) * fourth_share
    segment, living = segments(seq_lens[0], row_count)
    unscaled_value = hidden.astype(jnp.float32)
    inverse_root_mean = lax.rsqrt(jnp.mean(unscaled_value * unscaled_value, axis=1) + EPS)
    normalized_input = unscaled_value * inverse_root_mean[:, None]
    normalized_input_rows = lax.dynamic_slice_in_dim(
        normalized_input, index_of_row * width_of_row, width_of_row, 1
    )
    normalized_rows = (normalized_input_rows * rmsnorm_gain[None, :]).astype(jnp.bfloat16)
    z_sum = jnp.dot(normalized_rows, w_z, preferred_element_type=jnp.float32)
    x_sum = jnp.dot(normalized_rows, w_x, preferred_element_type=jnp.float32)
    dt_sum = jnp.dot(normalized_rows, w_dt, preferred_element_type=jnp.float32)
    z_in, x_in, dt_in = (
        lax.psum_scatter(z_sum, "row", scatter_dimension=1, tiled=True),
        lax.psum_scatter(x_sum, "row", scatter_dimension=1, tiled=True),
        lax.psum_scatter(dt_sum, "row", scatter_dimension=1, tiled=True),
    )
    bc_own = jnp.dot(normalized_rows, w_bc, preferred_element_type=jnp.float32)
    width_state = bc_own.shape[1]
    first_col = (col_index == 0).astype(jnp.float32)
    bc_wide = jnp.concatenate([bc_own * first_col, bc_own * (1.0 - first_col)], axis=1)
    bc_in = lax.psum(bc_wide, ("row", "col"))
    conv_flat = conv_x.reshape(conv_x.shape[0], -1)
    conv_bias_flat = conv_x_bias.reshape(-1)
    shift_flat = dt_bias.reshape(-1)
    alog_flat = a_log.reshape(-1)
    skip_flat = d_skip.reshape(-1)
    gain_flat = gate_gain.reshape(-1)

    def local_mix(
        x_part, bc_part, z_part, dt_part, conv_w, conv_b, bc_w, bc_b, dt_shift, a_logs, skips
    ):
        return mixer(
            x_part,
            bc_part,
            z_part,
            dt_part,
            conv_w,
            conv_b,
            bc_w,
            bc_b,
            dt_shift,
            a_logs,
            skips,
            segment,
            living,
        )

    mixed, pull = jax.vjp(
        local_mix,
        x_in,
        bc_in,
        z_in,
        dt_in,
        conv_flat,
        conv_bias_flat,
        conv_bc,
        conv_bc_bias,
        shift_flat,
        alog_flat,
        skip_flat,
    )
    gate_total = lax.psum(jnp.sum(mixed * mixed, axis=1), ("row", "col"))
    inv_gate = lax.rsqrt(gate_total / E + EPS)
    gated = (mixed * inv_gate[:, None] * gain_flat[None, :]).astype(jnp.bfloat16)
    gated_rows = lax.all_gather(gated, "row", axis=1, tiled=True)
    out_part = jnp.dot(gated_rows, w_out, preferred_element_type=jnp.float32)
    out_sum = lax.psum_scatter(
        out_part.astype(jnp.bfloat16), "col", scatter_dimension=1, tiled=True
    ).astype(jnp.float32)
    plain_own = lax.dynamic_slice_in_dim(unscaled_value, local_begin, fourth_share, 1)
    block_out = (plain_own + out_sum).astype(jnp.bfloat16)
    grad_part = jnp.dot(out_grad, w_out.T, preferred_element_type=jnp.float32)
    d_gated = lax.psum_scatter(grad_part, "row", scatter_dimension=1, tiled=True)
    grad_w_out = jnp.dot(gated_rows.T, out_grad, preferred_element_type=jnp.float32)
    grad_gate = jnp.sum(d_gated * mixed * inv_gate[:, None], axis=0)
    inner = lax.psum(jnp.sum(mixed * gain_flat[None, :] * d_gated, axis=1), ("row", "col"))
    d_mixed = (
        inv_gate[:, None] * gain_flat[None, :] * d_gated
        - mixed * (inv_gate**3 / E)[:, None] * inner[:, None]
    )
    (
        grad_x,
        grad_bc,
        grad_z,
        grad_dt,
        grad_cw,
        grad_cb,
        grad_bw,
        grad_bb,
        grad_shift,
        grad_alog,
        grad_skip,
    ) = pull(d_mixed)
    bc_full, grad_bw, grad_bb = lax.psum((grad_bc, grad_bw, grad_bb), ("row", "col"))
    z_rows, x_rows, dt_rows = (
        lax.all_gather(grad_z.astype(jnp.bfloat16), "row", axis=1, tiled=True),
        lax.all_gather(grad_x.astype(jnp.bfloat16), "row", axis=1, tiled=True),
        lax.all_gather(grad_dt.astype(jnp.bfloat16), "row", axis=1, tiled=True),
    )
    bc_round = lax.dynamic_slice_in_dim(bc_full, col_index * width_state, width_state, 1).astype(
        jnp.bfloat16
    )
    back_part = (
        jnp.dot(z_rows, w_z.T, preferred_element_type=jnp.float32)
        + jnp.dot(x_rows, w_x.T, preferred_element_type=jnp.float32)
        + jnp.dot(dt_rows, w_dt.T, preferred_element_type=jnp.float32)
        + jnp.dot(bc_round, w_bc.T, preferred_element_type=jnp.float32)
    )
    local_backward = lax.psum_scatter(back_part, "col", scatter_dimension=1, tiled=True)
    local_normalized_input = lax.dynamic_slice_in_dim(
        normalized_input, local_begin, fourth_share, 1
    )
    gain_own = lax.dynamic_slice_in_dim(rmsnorm_gain, col_index * fourth_share, fourth_share, 0)
    scaled_value = local_backward * gain_own[None, :]
    scaled_total_sum = lax.psum(
        jnp.sum(scaled_value * local_normalized_input, axis=1), ("row", "col")
    )
    local_incoming_gradient = lax.dynamic_slice_in_dim(
        out_grad, col_index * fourth_share, fourth_share, 1
    ).astype(jnp.float32)
    hidden_input_gradient = (
        local_incoming_gradient
        + inverse_root_mean[:, None]
        * (scaled_value - local_normalized_input * (scaled_total_sum / MODEL_WIDTH)[:, None])
    ).astype(jnp.bfloat16)
    norm_gradient = jnp.sum(local_backward * local_normalized_input, axis=0)
    grad_wz = jnp.dot(normalized_rows.T, z_rows, preferred_element_type=jnp.float32)
    grad_wx = jnp.dot(normalized_rows.T, x_rows, preferred_element_type=jnp.float32)
    grad_wbc = jnp.dot(normalized_rows.T, bc_round, preferred_element_type=jnp.float32)
    grad_wdt = jnp.dot(normalized_rows.T, dt_rows, preferred_element_type=jnp.float32)
    (
        norm_gradient,
        grad_wz,
        grad_wx,
        grad_wbc,
        grad_wdt,
        grad_cw,
        grad_cb,
        grad_bw,
        grad_bb,
        grad_shift,
        grad_alog,
        grad_skip,
        grad_gate,
        grad_w_out,
    ) = lax.psum(
        (
            norm_gradient,
            grad_wz,
            grad_wx,
            grad_wbc,
            grad_wdt,
            grad_cw,
            grad_cb,
            grad_bw,
            grad_bb,
            grad_shift,
            grad_alog,
            grad_skip,
            grad_gate,
            grad_w_out,
        ),
        "dp",
    )
    return (
        block_out,
        hidden_input_gradient,
        norm_gradient,
        grad_wz,
        grad_wx,
        grad_wbc,
        grad_wdt,
        grad_cw.reshape(conv_x.shape),
        grad_cb.reshape(conv_x_bias.shape),
        grad_bw,
        grad_bb,
        grad_shift.reshape(dt_bias.shape),
        grad_alog.reshape(a_log.shape),
        grad_skip.reshape(d_skip.shape),
        grad_gate.reshape(gate_gain.shape),
        grad_w_out,
    )


def solution(mesh):
    return jax.shard_map(
        per_device,
        mesh=mesh,
        in_specs=(
            P("dp", None),
            P("dp", "row"),
            P("dp", None),
            P("row"),
            P("row", "col"),
            P("row", "col"),
            P("row", "col"),
            P("row", "col"),
            P(None, "col", "row"),
            P("col", "row"),
            P(),
            P(),
            P("col", "row"),
            P("col", "row"),
            P("col", "row"),
            P("col", "row"),
            P("col", "row"),
        ),
        out_specs=(
            P("dp", ("row", "col")),
            P("dp", ("row", "col")),
            P(("row", "col")),
            P("row", "col"),
            P("row", "col"),
            P("row", "col"),
            P("row", "col"),
            P(None, "col", "row"),
            P("col", "row"),
            P(),
            P(),
            P("col", "row"),
            P("col", "row"),
            P("col", "row"),
            P("col", "row"),
            P("col", "row"),
        ),
        check_vma=False,
    )
```

profile of v0, /device:TPU:0, one launch (start us, length us, event | category | flops | bytes accessed | tf_op | source)
XLA Modules:
  0.0 723.2 jit_solution(3955127490219915827)
XLA Ops:
  32.6 48.0 %all-reduce.33.cloned.1.call-done = f32[768,256]{0,1:T(8,128)} async-done(((f32[768,256]{0,1:T(8,128)}), f32[768,256]{0,1:T(8,128)}) %all-reduce.33.cloned.1.call-update) | async-done | bytes 786448 | tf_op jit(solution)/shard_map/psum | solution.py:160
  80.6 4.0 fusion.142
  86.6 5.5 fusion.138
  103.8 99.0 %while.87 = (s32[]{:T(128)}, f32[8,64,128]{2,1,0:T(8,128)S(1)}, s32[]{:T(128)}, f32[3,256,8,64]{1,3,2,0:T(8,128)}, f32[3,256,8]{1,2,0:T(8,128)}, /*index=5*/pred...) while((s32[]{:T(128)}, f32[8,64,128]{2,1,0:T(8,128)S(1)}, ...), condition=%wide.region_9.10_spmd.clone, body=%wide.region_6.0_spmd.clone.sunk | while | flops 911886400 | bytes 17060204 | solution.py:75
  202.8 3.9 copy.126
  210.5 4.5 multiply_reduce_fusion.9
  215.0 5.7 psum.148
  223.8 5.7 psum.149
  229.6 5.6 multiply_reduce_fusion.3
  244.5 116.9 %while.88 = (s32[]{:T(128)}, f32[8]{0:T(128)}, f32[8,64,128]{2,1,0:T(8,128)S(1)}, f32[3,256,8,64]{1,3,2,0:T(8,128)}, f32[3,256,128]{2,1,0:T(8,128)}, /*index=5*/...) while((s32[]{:T(128)}, f32[8]{0:T(128)}, ...), condition=%wide.region_29.30_spmd.clone, body=%wide.region_17.29_spmd.clone.sunk | while | flops 1818392576 | bytes 19684116 | solution.py:75
  260.9 5.4 fusion.248
  299.3 5.4 fusion.248
  338.5 5.4 fusion.248
  365.0 3.9 reshape.596
  368.9 4.9 multiply_reduce_fusion.7
  386.0 15.9 %all-gather.4.cloned.1.call-done = bf16[768,1024]{1,0:T(8,128)(2,1)} async-done(((bf16[768,512]{1,0:T(8,128)(2,1)}), bf16[768,1024]{1,0:T(8,128)(2,1)}) %all-gather.4.cloned.1.call-update) | async-done | bytes 1572880 | tf_op jit(solution)/shard_map/all_gather | solution.py:204
  405.3 30.5 %all-reduce.36 = bf16[768,256]{0,1:T(8,128)(2,1)S(1)} all-reduce(f32[768,256]{0,1:T(8,128)S(1)} %get-tuple-element.1932), channel_id=1, replica_groups=mesh['dp'=8,'row'=2,'col'=2] {'row','col'}, use_global_device_ids=true, to_apply=%region_30.31 | all-reduce | flops 196608 | bytes 1179648 | tf_op jit(solution)/shard_map/psum | solution.py:233
  436.1 4.4 all_gather.15
  440.9 3.9 fusion.171
  444.7 23.9 %all-gather.6.cloned.1.call-done = bf16[768,1024]{1,0:T(8,128)(2,1)} async-done(((bf16[768,512]{1,0:T(8,128)(2,1)}), bf16[768,1024]{1,0:T(8,128)(2,1)}) %all-gather.6.cloned.1.call-update) | async-done | bytes 1572880 | tf_op jit(solution)/shard_map/all_gather | solution.py:235
  475.4 3.8 fusion.173
  491.8 6.0 all-reduce.28
  497.8 41.6 %all-reduce.26 = (f32[256]{0:T(256)}, f32[512,16]{0,1:T(8,128)}, f32[4,1,512]{2,1,0:T(1,128)}, f32[1,512]{1,0:T(1,128)}, f32[4,256]{1,0:T(4,128)}, /*index=5*/f3...) all-reduce(f32[256]{0:T(256)S(1)} %get-tuple-element.1717, ...), channel_id=1, replica_groups=mesh['dp'=8,'row'=2,'col'=2] {'dp'}, use_global_device_ids=true, to_apply=%region_35.36 | all-reduce | flops 12824 | bytes 102592 | tf_op jit(solution)/shard_map/psum | solution.py:285
  541.6 166.7 %all-reduce.35.cloned.1.call-done = (f32[512,1024]{1,0:T(8,128)}, f32[512,1024]{1,0:T(8,128)}, f32[512,128]{1,0:T(8,128)}, f32[1024,512]{1,0:T(8,128)}) async-done(((f32[512,1024]{1,0:T(8,128)}, f32[512,1024]{1,0:T(8,128)}, f32[512,128]{1,0:T(8,128)}, f32[1024,512]{1,0:T(8,128)}), (f32[512,1024]{1,0:T(8,128)}, f32[512,1024]{1,0:T(8,128)}, f32[512,128]{1,0:T(8,128)}, ...) | async-done | bytes 6553616 | tf_op jit(solution)/shard_map/psum | solution.py:285
  (490 shorter events, 297.2 us)
Async XLA Ops:
  8.0 23.1 %reduce-scatter.7.cloned.1.call-start = ((), (), s32[]{:S(2)}) async-start(), calls=%async_computation.6 | async-start | bytes 73728 | tf_op jit(solution)/shard_map/reduce_scatter | solution.py:154
  15.2 65.4 %all-reduce.33.cloned.1.call-start = ((), (), s32[]{:S(2)}) async-start(), calls=%async_computation.8 | async-start | bytes 1572864 | tf_op jit(solution)/shard_map/psum | solution.py:160
  16.7 69.9 %reduce-scatter.9.cloned.1.call-start = ((), (), s32[]{:S(2)}) async-start(), calls=%async_computation.7 | async-start | bytes 4718592 | tf_op jit(solution)/shard_map/reduce_scatter | solution.py:153
  19.9 190.5 %reduce-scatter.11.cloned.1.call-start = ((), (), s32[]{:S(2)}) async-start(), calls=%async_computation.9 | async-start | bytes 4718592 | tf_op jit(solution)/shard_map/reduce_scatter | solution.py:152
  23.8 197.0 %reduce-scatter.15.cloned.1.call-start = ((), (), s32[]{:S(2)}) async-start(), calls=%async_computation.12 | async-start | bytes 4718592 | tf_op jit(solution)/shard_map/reduce_scatter | solution.py:212
  27.7 52.9 %copy-start.75 = (f32[256]{0:T(256)S(1)}, f32[256]{0:T(256)}, u32[]{:S(2)}) copy-start(f32[256]{0:T(256)} %param.32) | copy-start | bytes 3076
  27.7 374.1 %all-gather.4.cloned.1.call-start = ((), (), s32[]{:S(2)}) async-start(), calls=%async_computation.10 | async-start | bytes 2359296 | tf_op jit(solution)/shard_map/all_gather | solution.py:204
  28.6 56.0 %copy-start.57 = (f32[1,256]{1,0:T(1,128)}, f32[1,256]{1,0:T(1,128)S(1)}, u32[]{:S(2)}) copy-start(f32[1,256]{1,0:T(1,128)S(1)} %get-tuple-element.1945) | copy-start | bytes 3076
  28.6 56.0 %copy-start.59 = (f32[1,256]{1,0:T(1,128)}, f32[1,256]{1,0:T(1,128)S(1)}, u32[]{:S(2)}) copy-start(f32[1,256]{1,0:T(1,128)S(1)} %get-tuple-element.1947) | copy-start | bytes 3076
  28.6 56.0 %copy-start.61 = (f32[1,256]{1,0:T(1,128)}, f32[1,256]{1,0:T(1,128)S(1)}, u32[]{:S(2)}) copy-start(f32[1,256]{1,0:T(1,128)S(1)} %get-tuple-element.1946) | copy-start | bytes 3076
  28.6 56.0 %copy-start.63 = (f32[1,256]{1,0:T(1,128)}, f32[1,256]{1,0:T(1,128)S(1)}, u32[]{:S(2)}) copy-start(f32[1,256]{1,0:T(1,128)S(1)} %get-tuple-element.1948) | copy-start | bytes 3076
  28.7 57.9 %copy-start.48 = (f32[1,1,512]{2,1,0:T(1,128)}, f32[1,1,512]{2,1,0:T(1,128)S(1)}, u32[]{:S(2)}) copy-start(f32[1,1,512]{2,1,0:T(1,128)S(1)} %get-tuple-element.1939) | copy-start | bytes 6148
  28.7 57.9 %copy-start.50 = (f32[1,1,512]{2,1,0:T(1,128)}, f32[1,1,512]{2,1,0:T(1,128)S(1)}, u32[]{:S(2)}) copy-start(f32[1,1,512]{2,1,0:T(1,128)S(1)} %get-tuple-element.1941) | copy-start | bytes 6148
  28.7 57.9 %copy-start.52 = (f32[1,1,512]{2,1,0:T(1,128)}, f32[1,1,512]{2,1,0:T(1,128)S(1)}, u32[]{:S(2)}) copy-start(f32[1,1,512]{2,1,0:T(1,128)S(1)} %get-tuple-element.1940) | copy-start | bytes 6148
  28.7 57.9 %copy-start.54 = (f32[1,1,512]{2,1,0:T(1,128)}, f32[1,1,512]{2,1,0:T(1,128)S(1)}, u32[]{:S(2)}) copy-start(f32[1,1,512]{2,1,0:T(1,128)S(1)} %get-tuple-element.1942) | copy-start | bytes 6148
  31.1 55.4 %copy-start.32 = (f32[768]{0:T(1024)}, f32[768]{0:T(1024)S(1)}, u32[]{:S(2)}) copy-start(f32[768]{0:T(1024)S(1)} %get-tuple-element.1949) | copy-start | bytes 9220
  31.1 55.4 %copy-start.34 = (f32[768]{0:T(1024)}, f32[768]{0:T(1024)S(1)}, u32[]{:S(2)}) copy-start(f32[768]{0:T(1024)S(1)} %get-tuple-element.1952) | copy-start | bytes 9220
  31.1 55.4 %copy-start.36 = (f32[768]{0:T(1024)}, f32[768]{0:T(1024)S(1)}, u32[]{:S(2)}) copy-start(f32[768]{0:T(1024)S(1)} %get-tuple-element.1951) | copy-start | bytes 9220
  373.8 67.0 %all-gather.8.cloned.1.call-start = ((), (), s32[]{:S(2)}) async-start(), calls=%async_computation.14 | async-start | bytes 2359296 | tf_op jit(solution)/shard_map/all_gather | solution.py:236
  381.3 87.4 %all-gather.6.cloned.1.call-start = ((), (), s32[]{:S(2)}) async-start(), calls=%async_computation.13 | async-start | bytes 2359296 | tf_op jit(solution)/shard_map/all_gather | solution.py:235
  383.0 105.0 %reduce-scatter.13.cloned.1.call-start = ((), (), s32[]{:S(2)}) async-start(), calls=%async_computation.11 | async-start | bytes 1179648 | tf_op jit(solution)/shard_map/reduce_scatter | solution.py:206
  405.2 84.9 %reduce-scatter.17.cloned.1.call-start = ((), (), s32[]{:S(2)}) async-start(), calls=%async_computation.15 | async-start | bytes 2359296 | tf_op jit(solution)/shard_map/reduce_scatter | solution.py:248
  473.2 235.1 %all-reduce.35.cloned.1.call-start = ((), (), s32[]{:S(2)}) async-start(), calls=%async_computation.16 | async-start | bytes 13107200 | tf_op jit(solution)/shard_map/psum | solution.py:285
  487.9 51.5 %copy-start.44 = (f32[768]{0:T(1024)S(1)}, f32[768]{0:T(1024)}, u32[]{:S(2)}) copy-start(f32[768]{0:T(1024)} %copy-done.43) | copy-start | bytes 9220
  (83 other events, 534.6 us)
Sparse Core Ops, SparseCore 0:
  15.3 12.7 reduce-scatter.6
  30.3 43.8 reduce-scatter.8
  76.4 43.4 reduce-scatter.10
  122.0 43.4 reduce-scatter.14
  373.9 27.8 all-gather.3
  403.8 35.9 all-gather.7
  441.4 27.2 all-gather.5
Sparse Core Ops, SparseCore 1:
  18.6 61.9 all-reduce.32
  405.3 8.1 reduce-scatter.12
  473.3 8.8 reduce-scatter.16
  487.8 220.4 all-reduce.34
where the time goes:
time: 731 us; the launch traced here: 723 us
  waiting for transfers between devices  255 us (35%)
  other arithmetic  138 us (19%)
  matrix products  112 us (15%)
  local copies, waits for them, and re-layouts  102 us (14%)
  blocking collectives  94 us (13%)
  between operations  16.9 us (2%)
    psum x1, waiting for transfers between devices, per_device(): lax.psum((norm_gradient, grad_wz, grad_wx, grad_wbc, grad_wdt, grad_cw, g...  167 us
    psum x1, waiting for transfers between devices, per_device(): bc_in = lax.psum(bc_wide, ('row', 'col'))  48 us
    psum x1, blocking collectives, per_device(): lax.psum((norm_gradient, grad_wz, grad_wx, grad_wbc, grad_wdt, grad_cw, g...  41.6 us
    dynamic_update_slice x27, other arithmetic, state_scan(): final_carry, outputs = lax.scan(advance, start, series)  38.9 us
    dot_general x9, matrix products, advance(): jnp.einsum('hts,shp->thp', decays * scores[None], weighted, precision=HIG...  37.5 us
    psum x1, blocking collectives, per_device(): lax.psum((grad_bc, grad_bw, grad_bb), ('row', 'col'))  30.5 us
    all_gather x1, waiting for transfers between devices, per_device(): lax.all_gather(grad_z.astype(jnp.bfloat16), 'row', axis=1, tiled=True)  23.9 us
    unnamed x156, local copies, waits for them, and re-layouts  21.1 us
  transfers between devices with their start and end apart: 11, of which 4 were waited for; matrix products, arithmetic and copies ran while one was open for 25% of the time, Pallas kernels for 0%

commit v1 on v0

v1 whole, which is shorter than its diff:
```python
import functools

import jax
import jax.numpy as jnp
from jax import lax
from jax.experimental import pallas as pl
from jax.experimental.pallas import tpu as pltpu
from jax.sharding import PartitionSpec as P

EPS = 1e-05
HIGHEST = lax.Precision.HIGHEST
F32 = jnp.float32
BF16 = jnp.bfloat16
LANES = 128
NEGATIVE = -1e30


def segments(lengths, row_count):
    ends = jnp.cumsum(lengths)
    places = jnp.arange(row_count, dtype=jnp.int32)
    segment = jnp.sum((places[:, None] >= ends[None, :]).astype(jnp.int32), axis=1)
    living = (segment < lengths.shape[0]).astype(F32)
    return (segment, living)


def depthwise(signal, weights, offset_bias, segment):
    row_count = signal.shape[0]
    total = offset_bias[None, :] + weights[0][None, :] * signal
    for offset in range(1, weights.shape[0]):
        moved = jnp.concatenate(
            [jnp.zeros((offset, signal.shape[1]), F32), signal[: row_count - offset]],
            axis=0,
        )
        earlier = jnp.concatenate(
            [jnp.full((offset,), -1, jnp.int32), segment[: row_count - offset]]
        )
        same_seq = (earlier == segment).astype(F32)
        total = total + weights[offset][None, :] * moved * same_seq[:, None]
    return total


def halves(a):
    high = a.astype(BF16)
    return high, (a - high.astype(F32)).astype(BF16)


def dot3(a, b, ca=1, cb=0):
    dims = (((ca,), (cb,)), ((), ()))
    ah, al = halves(a)
    bh, bl = halves(b)

    def one(u, v):
        return lax.dot_general(u, v, dims, preferred_element_type=F32)

    return one(ah, bh) + (one(ah, bl) + one(al, bh))


def dot6(a, b):
    return jnp.dot(a, b, precision=HIGHEST, preferred_element_type=F32)


def iota(shape, axis):
    return lax.broadcasted_iota(jnp.int32, shape, axis)


def decays_of(dt, dt_t, rate_row, rate_col, heads, width):
    rows = dt.shape[0]
    lower = (iota((rows, rows), 0) >= iota((rows, rows), 1)).astype(F32)
    upper = (iota((rows, rows), 0) <= iota((rows, rows), 1)).astype(F32)
    logs = dot6(lower, -dt * rate_row)
    logs_t = dot6(-dt_t * rate_col, upper)
    spread = (iota((heads, width), 0) == iota((heads, width), 1) // (width // heads)).astype(F32)
    return logs, logs_t, upper, spread


def scan_forward(x_ref, b_ref, c_ref, dt_ref, dtt_ref, sc_ref, sr_ref, aux_ref, rr_ref, rc_ref,
                 y_ref, st_ref, state):
    @pl.when(pl.program_id(0) == 0)
    def _():
        state[...] = jnp.zeros_like(state)

    st_ref[0] = state[...]
    rows, width = x_ref.shape
    heads = dt_ref.shape[1]
    each = width // heads
    x, b, c, dt = x_ref[...], b_ref[...], c_ref[...], dt_ref[...]
    logs, logs_t, upper, spread = decays_of(dt, dtt_ref[...], rr_ref[...], rc_ref[...], heads, width)
    keep, last = aux_ref[:, 0:1], aux_ref[:, 1:2]
    grown = dot6(jnp.exp(logs), spread)
    closing = dot6(jnp.exp(logs[rows - 1 :] - logs), spread) * last
    xw = x * dot6(dt, spread)
    before = state[...]
    carried = dot3(c, before) * (grown * keep)
    mask = jnp.logical_and(sc_ref[...] == sr_ref[...], iota((rows, rows), 0) >= iota((rows, rows), 1))
    scores = dot3(c, b, 1, 1)
    per = LANES // each
    lane = iota((rows, LANES), 1) // each
    for group in range(width // LANES):
        cols = slice(group * LANES, (group + 1) * LANES)
        total = carried[:, cols]
        for j in range(per):
            h = group * per + j
            gap = logs[:, h : h + 1] - logs_t[h : h + 1, :]
            weight = jnp.exp(jnp.where(mask, gap, NEGATIVE)) * scores
            total = total + dot3(weight, jnp.where(lane == j, xw[:, cols], 0.0))
        y_ref[:, cols] = total
    held = grown[rows - 1 :] * keep[rows - 1 :]
    state[...] = before * held + dot3(b, xw * closing, 0, 0)


def scan_backward(x_ref, b_ref, c_ref, dt_ref, dtt_ref, sc_ref, sr_ref, aux_ref, rr_ref, rc_ref,
                  y_ref, st_ref, dy_ref, dx_ref, db_ref, dc_ref, ddt_ref, da_ref, dstate):
    @pl.when(pl.program_id(0) == 0)
    def _():
        dstate[...] = jnp.zeros_like(dstate)
        da_ref[...] = jnp.zeros_like(da_ref)

    rows, width = x_ref.shape
    heads = dt_ref.shape[1]
    each = width // heads
    x, b, c, dt, dy = x_ref[...], b_ref[...], c_ref[...], dt_ref[...], dy_ref[...]
    logs, logs_t, upper, spread = decays_of(dt, dtt_ref[...], rr_ref[...], rc_ref[...], heads, width)
    keep, last = aux_ref[:, 0:1], aux_ref[:, 1:2]
    grown = dot6(jnp.exp(logs), spread)
    closing = dot6(jnp.exp(logs[rows - 1 :] - logs), spread) * last
    dt_wide = dot6(dt, spread)
    xw = x * dt_wide
    before, after = st_ref[0], dstate[...]
    held = grown[rows - 1 :] * keep[rows - 1 :]
    u = dy * (grown * keep)
    dc = dot3(u, before, 1, 1)
    v = dot3(b, after)
    xc = xw * closing
    db = dot3(xc, after, 1, 1)
    tail = jnp.sum(before * after, axis=0, keepdims=True) * held + jnp.sum(v * xc, axis=0, keepdims=True)
    dstate[...] = dot3(c, u, 0, 0) + after * held
    mask = jnp.logical_and(sc_ref[...] == sr_ref[...], iota((rows, rows), 0) <= iota((rows, rows), 1))
    scores = dot3(b, c, 1, 1)
    per = LANES // each
    lane = iota((rows, LANES), 1) // each
    dscores = jnp.zeros((rows, rows), F32)
    pieces = []
    for group in range(width // LANES):
        cols = slice(group * LANES, (group + 1) * LANES)
        total = v[:, cols] * closing[:, cols]
        for j in range(per):
            h = group * per + j
            gap = logs_t[h : h + 1, :] - logs[:, h : h + 1]
            decay = jnp.exp(jnp.where(mask, gap, NEGATIVE))
            dyj = jnp.where(lane == j, dy[:, cols], 0.0)
            total = total + dot3(decay * scores, dyj)
            dscores = dscores + dot3(xw[:, cols], dyj, 1, 1) * decay
        pieces.append(total)
    dxw = jnp.concatenate(pieces, axis=1)
    db_ref[...] = db + dot3(dscores, c)
    dc_ref[...] = dc + dot3(dscores, b, 0, 0)
    gather = (iota((width, heads), 0) // each == iota((width, heads), 1)).astype(F32)
    wide = dy * y_ref[...] - xw * dxw
    wide = wide + jnp.where(iota((rows, width), 0) == rows - 1, tail, 0.0)
    dneg = dot6(upper, dot6(wide, gather))
    ddt_ref[...] = dot6(dxw * x, gather) - dneg * rr_ref[...]
    da_ref[...] = da_ref[...] - jnp.sum(dt * dneg, axis=0, keepdims=True)
    dx_ref[...] = dxw * dt_wide


def scan_specs(rows, width, state, heads, count, backward):
    def at(i):
        return count - 1 - i if backward else i

    tall = lambda n: pl.BlockSpec((rows, n), lambda i: (at(i), 0))
    flat = lambda n: pl.BlockSpec((n, rows), lambda i: (0, at(i)))
    fixed = lambda a, b: pl.BlockSpec((a, b), lambda i: (0, 0))
    ins = [tall(width), tall(state), tall(state), tall(heads), flat(heads), tall(1), flat(1),
           tall(2), fixed(1, heads), fixed(heads, 1)]
    states = pl.BlockSpec((1, state, width), lambda i: (at(i), 0, 0))
    return ins, tall, fixed, states


def scan_operands(x, b, c, dt, rates, segment, block):
    row_count = x.shape[0]
    series = segment.reshape(row_count // block, block)
    closing = series[:, -1:]
    previous = jnp.concatenate([jnp.full((1, 1), -1, jnp.int32), closing[:-1]], axis=0)
    aux = jnp.stack(
        [(series == previous).astype(F32).reshape(-1), (series == closing).astype(F32).reshape(-1)],
        axis=1,
    )
    return (x, b, c, dt, dt.T, segment[:, None], segment[None, :], aux, rates[None, :], rates[:, None])


@functools.partial(jax.custom_vjp, nondiff_argnums=(6,))
def state_scan(x, b, c, dt, rates, segment, block):
    return scan_fwd(x, b, c, dt, rates, segment, block)[0]


def scan_fwd(x, b, c, dt, rates, segment, block):
    row_count, width = x.shape
    state, heads = b.shape[1], dt.shape[1]
    count = row_count // block
    ins, tall, fixed, states = scan_specs(block, width, state, heads, count, False)
    y, kept = pl.pallas_call(
        scan_forward,
        grid=(count,),
        in_specs=ins,
        out_specs=[tall(width), states],
        out_shape=[
            jax.ShapeDtypeStruct((row_count, width), F32),
            jax.ShapeDtypeStruct((count, state, width), F32),
        ],
        scratch_shapes=[pltpu.VMEM((state, width), F32)],
        compiler_params=pltpu.CompilerParams(vmem_limit_bytes=48 * 1024 * 1024),
        cost_estimate=pl.CostEstimate(flops=2_000_000_000, bytes_accessed=6_000_000, transcendentals=0),
        name="scan_forward",
    )(*scan_operands(x, b, c, dt, rates, segment, block))
    return y, (x, b, c, dt, rates, segment, y, kept)


def scan_bwd(block, saved, dy):
    x, b, c, dt, rates, segment, y, kept = saved
    row_count, width = x.shape
    state, heads = b.shape[1], dt.shape[1]
    count = row_count // block
    ins, tall, fixed, states = scan_specs(block, width, state, heads, count, True)
    dx, db, dc, ddt, da = pl.pallas_call(
        scan_backward,
        grid=(count,),
        in_specs=ins + [tall(width), states, tall(width)],
        out_specs=[tall(width), tall(state), tall(state), tall(heads), fixed(1, heads)],
        out_shape=[
            jax.ShapeDtypeStruct((row_count, width), F32),
            jax.ShapeDtypeStruct((row_count, state), F32),
            jax.ShapeDtypeStruct((row_count, state), F32),
            jax.ShapeDtypeStruct((row_count, heads), F32),
            jax.ShapeDtypeStruct((1, heads), F32),
        ],
        scratch_shapes=[pltpu.VMEM((state, width), F32)],
        compiler_params=pltpu.CompilerParams(vmem_limit_bytes=48 * 1024 * 1024),
        cost_estimate=pl.CostEstimate(flops=6_000_000_000, bytes_accessed=10_000_000, transcendentals=0),
        name="scan_backward",
    )(*scan_operands(x, b, c, dt, rates, segment, block), y, kept, dy)
    return dx, db, dc, ddt, da[0], None


state_scan.defvjp(scan_fwd, scan_bwd)


def mixer(x_part, bc_part, z_part, dt_part, conv_w, conv_b, bc_w, bc_b, dt_shift, a_logs, skips,
          segment, living):
    row_count, width = x_part.shape
    heads = dt_shift.shape[0]
    x_act = jax.nn.silu(depthwise(x_part, conv_w, conv_b, segment))
    bc_act = jax.nn.silu(depthwise(bc_part, bc_w, bc_b, segment))
    state = bc_act.shape[1] // 2
    steps = jax.nn.softplus(dt_part + dt_shift[None, :])
    block = min(row_count, 256)
    scanned = state_scan(
        x_act, bc_act[:, :state], bc_act[:, state:], steps, jnp.exp(a_logs), segment, block
    )
    scanned = scanned + jnp.repeat(skips, width // heads)[None, :] * x_act
    return scanned * jax.nn.silu(z_part) * living[:, None]


def swap(value, axis):
    count = lax.axis_size(axis)
    return lax.ppermute(value, axis, [(i, (i + 1) % count) for i in range(count)])


def part(value, index, axis):
    size = value.shape[axis] // 2
    return lax.dynamic_slice_in_dim(value, index * size, size, axis)


def ordered(own, other, index, axis):
    first = index == 0
    return jnp.concatenate([jnp.where(first, own, other), jnp.where(first, other, own)], axis=axis)


def dot(a, b):
    return jnp.dot(a, b, preferred_element_type=F32)


def per_device(hidden, out_grad, seq_lens, rmsnorm_gain, w_z, w_x, w_bc, w_dt, conv_x, conv_x_bias,
               conv_bc, conv_bc_bias, dt_bias, a_log, d_skip, gate_gain, w_out):
    row_count, model_width = hidden.shape
    row, col = lax.axis_index("row"), lax.axis_index("col")
    batches = lax.axis_size("dp")
    shares = lax.axis_size("row") * lax.axis_size("col")
    inner_width = w_z.shape[1] * lax.axis_size("col")
    half = model_width // 2

    def own_heads(weight, axis):
        mine = part(weight, row, axis)
        theirs = swap(part(weight, 1 - row, axis), "row")
        return jnp.concatenate([mine, theirs], axis=1 - axis)

    wx = own_heads(w_x, 1)
    wbc_cols = ordered(w_bc, swap(w_bc, "col"), col, 1)
    wbc = jnp.concatenate([wbc_cols, swap(wbc_cols, "row")], axis=0)
    wdt = own_heads(w_dt, 1)
    gain = jnp.concatenate([rmsnorm_gain, swap(rmsnorm_gain, "row")])
    wz = own_heads(w_z, 1)
    incoming = jnp.concatenate([out_grad, swap(out_grad, "row")], axis=1)
    wo = own_heads(w_out, 0)

    segment, living = segments(seq_lens[0], row_count)
    whole = hidden.astype(F32)
    whole = jnp.where(row == 0, whole, jnp.concatenate([whole[:, half:], whole[:, :half]], axis=1))
    scale = lax.rsqrt(jnp.mean(whole * whole, axis=1) + EPS)
    xhat = whole * scale[:, None]
    normed = (xhat * gain[None, :]).astype(BF16)
    x_in = dot(normed, wx)
    bc_in = dot(normed, wbc)
    dt_in = dot(normed, wdt)
    z_in = dot(normed, wz)
    gain_flat = gate_gain.reshape(-1)

    def local_mix(*parts):
        return mixer(*parts, segment, living)

    mixed, pull = jax.vjp(
        local_mix, x_in, bc_in, z_in, dt_in, conv_x.reshape(conv_x.shape[0], -1),
        conv_x_bias.reshape(-1), conv_bc, conv_bc_bias, dt_bias.reshape(-1), a_log.reshape(-1),
        d_skip.reshape(-1),
    )
    d_gated = dot(incoming, wo.T)
    sums = jnp.stack(
        [jnp.sum(mixed * mixed, axis=1), jnp.sum(mixed * gain_flat[None, :] * d_gated, axis=1)]
    )
    sums = lax.psum(sums, ("row", "col"))
    inv_gate = lax.rsqrt(sums[0] / inner_width + EPS)
    inner = sums[1]
    gated = (mixed * inv_gate[:, None] * gain_flat[None, :]).astype(BF16)
    d_mixed = (
        inv_gate[:, None] * gain_flat[None, :] * d_gated
        - mixed * (inv_gate**3 / inner_width)[:, None] * inner[:, None]
    )

    def scattered(partial):
        kept = partial[:, :half] + swap(partial[:, half:].astype(BF16), "row").astype(F32)
        return part(kept, col, 1) + swap(part(kept, 1 - col, 1).astype(BF16), "col").astype(F32)

    grad_wo = dot(gated.T, incoming).astype(BF16)
    wo_piece = lax.psum_scatter(grad_wo, "dp", scatter_dimension=0, tiled=True)
    wo_pair = jnp.stack([wo_piece[:, :half], swap(wo_piece[:, half:], "row")])
    wo_pair = jnp.where(row == 0, wo_pair, wo_pair[::-1])
    wo_all = lax.all_gather(wo_pair, "dp", axis=1, tiled=True)
    grad_w_out = wo_all.reshape(-1, half).astype(F32)

    out_sum = scattered(dot(gated, wo))
    block_out = (part(whole[:, :half], col, 1) + out_sum).astype(BF16)
    grad_gate = jnp.sum(d_gated * mixed * inv_gate[:, None], axis=0)

    (grad_x, grad_bc, grad_z, grad_dt, grad_cw, grad_cb, grad_bw, grad_bb, grad_shift, grad_alog,
     grad_skip) = pull(d_mixed)
    dz, dx, ddt, dbc = (v.astype(BF16) for v in (grad_z, grad_x, grad_dt, grad_bc))

    steps = ddt.shape[1]
    grads = jnp.concatenate(
        [dz, dx, dbc, ddt, jnp.zeros((row_count, LANES - steps), BF16)], axis=1
    )
    big = dot(normed.T, grads).astype(BF16)
    wide = big.shape[1]
    big = big.reshape(2, batches, -1, wide).transpose(1, 0, 2, 3).reshape(-1, wide)
    piece = lax.psum_scatter(big, "dp", scatter_dimension=0, tiled=True)
    piece = piece.reshape(2, -1, wide)
    mine, theirs = piece[0], swap(piece[1], "row")
    nz, nbc = dz.shape[1], dbc.shape[1]
    bc_sum = (mine[:, 2 * nz : 2 * nz + nbc].astype(F32)
              + theirs[:, 2 * nz : 2 * nz + nbc].astype(F32))
    bc_sum = part(bc_sum, col, 1) + swap(part(bc_sum, 1 - col, 1).astype(BF16), "col").astype(F32)
    pieces = jnp.concatenate(
        [
            ordered(mine[:, :nz], theirs[:, :nz], row, 1),
            ordered(mine[:, nz : 2 * nz], theirs[:, nz : 2 * nz], row, 1),
            bc_sum.astype(BF16),
            jnp.where(row == 0, mine[:, 2 * nz + nbc :], theirs[:, 2 * nz + nbc :]),
            jnp.where(row == 0, theirs[:, 2 * nz + nbc :], mine[:, 2 * nz + nbc :]),
        ],
        axis=1,
    )
    whole_grads = lax.all_gather(pieces, "dp", axis=0, tiled=True)
    grad_wz = whole_grads[:, : 2 * nz].astype(F32)
    grad_wx = whole_grads[:, 2 * nz : 4 * nz].astype(F32)
    at = 4 * nz
    grad_wbc = whole_grads[:, at : at + nbc // 2].astype(F32)
    at = at + nbc // 2
    grad_wdt = jnp.concatenate(
        [whole_grads[:, at : at + steps], whole_grads[:, at + LANES : at + LANES + steps]], axis=1
    ).astype(F32)

    back = dot(dz, wz.T) + dot(dx, wx.T) + dot(ddt, wdt.T) + dot(dbc, wbc.T)
    d_normed = scattered(back)
    xhat_own = part(xhat[:, :half], col, 1)
    scaled = d_normed * part(rmsnorm_gain, col, 0)[None, :]
    total = lax.psum(jnp.sum(scaled * xhat_own, axis=1), ("row", "col"))
    hidden_input_gradient = (
        part(out_grad, col, 1).astype(F32)
        + scale[:, None] * (scaled - xhat_own * (total / model_width)[:, None])
    ).astype(BF16)
    norm_gradient = jnp.sum(d_normed * xhat_own, axis=0)

    (norm_gradient, grad_cw, grad_cb, grad_shift, grad_alog, grad_skip, grad_gate) = lax.psum(
        (norm_gradient, grad_cw, grad_cb, grad_shift, grad_alog, grad_skip, grad_gate), "dp"
    )
    grad_bw, grad_bb = lax.psum((grad_bw, grad_bb), ("dp", "row", "col"))
    return (
        block_out,
        hidden_input_gradient,
        norm_gradient,
        grad_wz,
        grad_wx,
        grad_wbc,
        grad_wdt,
        grad_cw.reshape(conv_x.shape),
        grad_cb.reshape(conv_x_bias.shape),
        grad_bw,
        grad_bb,
        grad_shift.reshape(dt_bias.shape),
        grad_alog.reshape(a_log.shape),
        grad_skip.reshape(d_skip.shape),
        grad_gate.reshape(gate_gain.shape),
        grad_w_out,
    )


def solution(mesh):
    return jax.shard_map(
        per_device,
        mesh=mesh,
        in_specs=(
            P("dp", None),
            P("dp", "row"),
            P("dp", None),
            P("row"),
            P("row", "col"),
            P("row", "col"),
            P("row", "col"),
            P("row", "col"),
            P(None, "col", "row"),
            P("col", "row"),
            P(),
            P(),
            P("col", "row"),
            P("col", "row"),
            P("col", "row"),
            P("col", "row"),
            P("col", "row"),
        ),
        out_specs=(
            P("dp", ("row", "col")),
            P("dp", ("row", "col")),
            P(("row", "col")),
            P("row", "col"),
            P("row", "col"),
            P("row", "col"),
            P("row", "col"),
            P(None, "col", "row"),
            P("col", "row"),
            P(),
            P(),
            P("col", "row"),
            P("col", "row"),
            P("col", "row"),
            P("col", "row"),
            P("col", "row"),
        ),
        check_vma=False,
    )
```

time: 731 us -> 424 us (0.58)
  waiting for transfers between devices: 255 us -> 148 us
  other arithmetic: 138 us -> 50 us
  matrix products: 112 us -> 28.1 us
  local copies, waits for them, and re-layouts: 102 us -> 36.5 us
  Pallas kernels: 0 us -> 33.1 us
  starting transfers between devices: 0.81 us -> 15.5 us
    psum x2 -> x0, waiting for transfers between devices: 215 us -> none  [the longest x1 167 us: per_device(): lax.psum((norm_gradient, grad_wz, grad_wx, grad_wbc, grad_wdt, grad_cw, g...]
    dot_general x51 -> x12, matrix products: 112 us -> 28.1 us  [dot(): return jnp.dot(a, b, preferred_element_type=F32)]
    reduce_scatter x6 -> x2, waiting for transfers between devices: 0.05 us -> 83 us  [the longest x1 67.4 us: per_device(): piece = lax.psum_scatter(big, 'dp', scatter_dimension=0, tiled=True)]
    ppermute x0 -> x15, waiting for transfers between devices: none -> 64.7 us  [swap(): lax.ppermute(value, axis, [(i, (i + 1) % count) for i in range(count)])]
    all_gather x3 -> x2, waiting for transfers between devices: 39.9 us -> 0.01 us  [the longest x1 0.01 us: per_device(): wo_all = lax.all_gather(wo_pair, 'dp', axis=1, tiled=True)]
    dynamic_update_slice x27 -> x0, other arithmetic: 38.9 us -> none  [state_scan(): final_carry, outputs = lax.scan(advance, start, series)]
    pallas_call x0 -> x2, Pallas kernels: none -> 33.1 us  [the longest x1 22.9 us: mixer(): state_scan(x_act, bc_act[:, :state], bc_act[:, state:], steps, jnp.exp(a_...]
    reduce_sum x18 -> x4, other arithmetic: 31.1 us -> 8.13 us  [the longest x2 6.11 us: mixer(): scanned = scanned + jnp.repeat(skips, width // heads)[None, :] * x_act]
  transfers between devices with their start and end apart: 11 -> 19, of which waited for: 4 -> 6; matrix products, arithmetic and copies ran while one was open for 25% -> 21% of each run, Pallas kernels for 0% -> 8%
where the time goes in v1:
time: 424 us; the launch traced here: 418 us
  waiting for transfers between devices  148 us (35%)
  blocking collectives  91.7 us (22%)
  other arithmetic  50 us (12%)
  local copies, waits for them, and re-layouts  36.5 us (9%)
  Pallas kernels  33.1 us (8%)
  matrix products  28.1 us (7%)
  between operations  15.6 us (4%)
  starting transfers between devices  15.5 us (4%)
    reduce_scatter x1, waiting for transfers between devices, per_device(): piece = lax.psum_scatter(big, 'dp', scatter_dimension=0, tiled=True)  67.4 us
    ppermute x15, waiting for transfers between devices, swap(): lax.ppermute(value, axis, [(i, (i + 1) % count) for i in range(count)])  64.7 us
    psum x1, blocking collectives, per_device(): grad_bw, grad_bb = lax.psum((grad_bw, grad_bb), ('dp', 'row', 'col'))  41.9 us
    psum x1, blocking collectives, per_device(): lax.psum((norm_gradient, grad_cw, grad_cb, grad_shift, grad_alog, grad_sk...  37.3 us
    dot_general x12, matrix products, dot(): return jnp.dot(a, b, preferred_element_type=F32)  28.1 us
    pallas_call x1, Pallas kernels, mixer(): state_scan(x_act, bc_act[:, :state], bc_act[:, state:], steps, jnp.exp(a_...  22.9 us
    reduce_scatter x1, waiting for transfers between devices, per_device(): wo_piece = lax.psum_scatter(grad_wo, 'dp', scatter_dimension=0, tiled=True)  15.7 us
    ppermute x15, starting transfers between devices, swap(): lax.ppermute(value, axis, [(i, (i + 1) % count) for i in range(count)])  15.1 us
  transfers between devices with their start and end apart: 19, of which 6 were waited for; matrix products, arithmetic and copies ran while one was open for 21% of the time, Pallas kernels for 8%

profile of v1, /device:TPU:0, one launch (start us, length us, event | category | flops | bytes accessed | tf_op | source)
XLA Modules:
  0.0 418.4 jit_solution(15531169195107209173)
XLA Ops:
  7.2 3.0 collective-permute-start
  13.6 2.3 constant_dynamic-slice_fusion.3
  31.0 2.8 multiply_convert_fusion
  40.8 30.6 %collective-permute-done.3 = bf16[512,256]{1,0:T(8,128)(2,1)S(1)} collective-permute-done((bf16[512,256]{1,0:T(8,128)(2,1)S(1)}, bf16[512,256]{1,0:T(8,128)(2,1)S(1)}, u32[]{:S(2)}, u32[]{:S(2)}) %collective-permute-start.3) | collective-permute-done | bytes 262176 | tf_op jit(solution)/shard_map/ppermute | solution.py:265
  81.0 10.2 %jvp_scan_forward_.1 = (f32[768,512]{1,0:T(8,128)S(1)}, f32[3,128,512]{2,1,0:T(8,128)S(1)}) custom-call(f32[768,512]{1,0:T(8,128)S(1)} %get-tuple-element.118.x_ref, f32[768,128]{1,0:T(8,128)S(1)} %get-tuple-element.145.b_ref, f32[768,128]{1,0:T(8,128)S(1)} %get-tuple-element.144.c_ref, f32[768,8]{1,0:T(8,128)S(1)} %copy-done.10, f32[8,768]{1,0:T(8,128)S(1)} %copy-done.8, ...), custom_call_target="tpu_custom_call" | custom-call | flops 2000000000 | bytes 6000000 | tf_op jit(solution)/shard_map/jvp(scan_forward)/pallas_call | solution.py:201
  91.3 2.5 fusion.14
  95.8 3.2 multiply_reduce_fusion.8
  99.1 6.6 %psum.77 = f32[2,768]{1,0:T(2,128)S(1)} all-reduce(f32[2,768]{1,0:T(2,128)S(1)} %pad_maximum_fusion.19), channel_id=1, replica_groups=mesh['dp'=8,'row'=2,'col'=2] {'row','col'}, use_global_device_ids=true, to_apply=%region_5.6 | all-reduce | flops 1536 | bytes 12288 | tf_op jit(solution)/shard_map/psum | solution.py:329
  106.9 4.1 convolution_convert_fusion.1
  111.2 5.5 %multiply_reduce_fusion.2 = (f32[512]{0:T(512)}, f32[768,512]{1,0:T(8,128)}, bf16[768,512]{1,0:T(8,128)(2,1)}, f32[512]{0:T(512)}) fusion(f32[768,512]{1,0:T(8,128)S(1)} %copy-done.22, f32[768,512]{1,0:T(8,128)} %copy-done.46, f32[768]{0:T(1024)} %get-tuple-element.161, f32[768]{0:T(1024)} %get-tuple-element.86, f32[768,512]{1,0:T(8,128)} %get-tuple-element.115, ...), kind=kLoop, calls=%fused_computation.20 | loop fusion | flops 11795456 | bytes 10244096 | tf_op jit(solution)/shard_map/transpose(jvp())/reduce_sum | solution.py:259
  116.8 22.9 %transpose_jvp_scan_backward__.1 = (f32[768,512]{1,0:T(8,128)S(1)}, f32[768,128]{1,0:T(8,128)S(1)}, f32[768,128]{1,0:T(8,128)S(1)}, f32[768,8]{1,0:T(8,128)S(1)}, f32[1,8]{1,0:T(1,128)S(1)}) custom-call(f32[768,512]{1,0:T(8,128)} %copy-done, f32[768,128]{1,0:T(8,128)S(1)} %copy-done.7, f32[768,128]{1,0:T(8,128)S(1)} %copy-done.5, f32[768,8]{1,0:T(8,128)S(1)} %copy-done.11, ...), custom_call_target="tpu_custom_call" | custom-call | flops 6000000000 | bytes 10000000 | tf_op jit(solution)/shard_map/transpose(jvp(scan_backward))/pallas_call | solution.py:256
  150.8 3.0 concatenate.93
  153.8 4.8 %convolution_convert_fusion = bf16[1024,1408]{1,0:T(8,128)(2,1)S(1)} fusion(bf16[768,1024]{1,0:T(8,128)(2,1)} %copy-done.44, bf16[768,1408]{1,0:T(8,128)(2,1)} %concatenate.93), kind=kOutput, calls=%fused_computation | convolution fusion | flops 2216034304 | bytes 6619136 | tf_op jit(solution)/shard_map/dot_general | solution.py:279
  160.6 15.7 %reduce-scatter.5.cloned.1.call-done = bf16[64,1024]{1,0:T(8,128)(2,1)} async-done(((bf16[512,1024]{1,0:T(8,128)(2,1)}), bf16[64,1024]{1,0:T(8,128)(2,1)}) %reduce-scatter.5.cloned.1.call-update) | async-done | bytes 131088 | tf_op jit(solution)/shard_map/reduce_scatter | solution.py:343
  183.7 67.4 %reduce-scatter.3.cloned.1.call-done = bf16[128,1408]{1,0:T(8,128)(2,1)} async-done(((bf16[1024,1408]{1,0:T(8,128)(2,1)}), bf16[128,1408]{1,0:T(8,128)(2,1)}) %reduce-scatter.3.cloned.1.call-update) | async-done | bytes 360464 | tf_op jit(solution)/shard_map/reduce_scatter | solution.py:364
  254.5 3.1 collective-permute-done.12
  275.6 15.7 %collective-permute-done.10 = bf16[768,512]{1,0:T(8,128)(2,1)S(1)} collective-permute-done((bf16[768,512]{1,0:T(8,128)(2,1)S(1)}, bf16[768,512]{1,0:T(8,128)(2,1)S(1)}, u32[]{:S(2)}, u32[]{:S(2)}) %collective-permute-start.10) | collective-permute-done | bytes 786464 | tf_op jit(solution)/shard_map/ppermute | solution.py:265
  292.4 15.3 %collective-permute-done.8 = bf16[768,512]{1,0:T(8,128)(2,1)S(1)} collective-permute-done((bf16[768,512]{1,0:T(8,128)(2,1)S(1)}, bf16[768,512]{1,0:T(8,128)(2,1)S(1)}, u32[]{:S(2)}, u32[]{:S(2)}) %collective-permute-start.8) | collective-permute-done | bytes 786464 | tf_op jit(solution)/shard_map/ppermute | solution.py:265
  309.9 41.9 %all-reduce.24 = (f32[4,256]{1,0:T(4,128)}, f32[256]{0:T(256)}) all-reduce(f32[4,256]{1,0:T(4,128)S(1)} %pad_add_fusion.2, f32[256]{0:T(256)} %get-tuple-element.84), channel_id=1, replica_groups=mesh['dp'=8,'row'=2,'col'=2] {'dp','row','col'}, use_global_device_ids=true, to_apply=%region_22.23 | all-reduce | flops 1280 | bytes 10240 | tf_op jit(solution)/shard_map/psum | solution.py:405
  354.6 37.3 %all-reduce.25 = (f32[256]{0:T(256)}, f32[4,1,512]{2,1,0:T(1,128)}, f32[1,512]{1,0:T(1,128)}, f32[1,8]{1,0:T(1,128)}, f32[1,8]{1,0:T(1,128)}, /*index=5*/f32[1,8]{1,0:T(1,128)}, f32[1,512]{1,0:T(1,128)}) all-reduce(f32[256]{0:T(256)} %get-tuple-element.78, ...), channel_id=1, replica_groups=mesh['dp'=8,'row'=2,'col'=2] {'dp'}, use_global_device_ids=true, to_apply=%region_9.10 | all-reduce | flops 3352 | bytes 26816 | tf_op jit(solution)/shard_map/psum | solution.py:402
  391.9 5.9 %psum.78 = f32[768]{0:T(1024)S(1)} all-reduce(f32[768]{0:T(1024)S(1)} %get-tuple-element.79), channel_id=1, replica_groups=mesh['dp'=8,'row'=2,'col'=2] {'row','col'}, use_global_device_ids=true, to_apply=%region_7.8 | all-reduce | flops 768 | bytes 6144 | tf_op jit(solution)/shard_map/psum | solution.py:395
  397.8 2.4 add_convert_fusion.3
  401.4 2.8 bitcast_convert_fusion
  407.6 4.0 slice_convert_fusion.2
  (370 shorter events, 89.8 us)
Async XLA Ops:
  7.2 169.0 %reduce-scatter.5.cloned.1.call-start = ((), (), s32[]{:S(2)}) async-start(), calls=%async_computation.4 | async-start | bytes 1179648 | tf_op jit(solution)/shard_map/reduce_scatter | solution.py:343
  7.2 21.0 %collective-permute-start = (f32[512]{0:T(512)}, f32[512]{0:T(512)}, u32[]{:S(2)}, u32[]{:S(2)}) collective-permute-start(f32[512]{0:T(512)} %param.20), channel_id=1, source_target_pairs={{0,2},{2,0},{1,3},{3,1},{4,6},{6,4},{5,7},{7,5},{8,10},{10,8},{9,1... | collective-permute-start | bytes 6152 | tf_op jit(solution)/shard_map/ppermute | solution.py:265
  11.6 23.5 %collective-permute-start.4 = (bf16[512,8]{0,1:T(8,128)(2,1)}, bf16[512,8]{0,1:T(8,128)(2,1)}, u32[]{:S(2)}, u32[]{:S(2)}) collective-permute-start(bf16[512,8]{0,1:T(8,128)(2,1)} %get-tuple-element.151), channel_id=1, source_target_pairs={{0,2},{2,0},{1,3},{3,1},{4,6},{6,4},{5,7},{7,5},{8,10},{10,8},{9,1... | collective-permute-start | bytes 24584 | tf_op jit(solution)/shard_map/ppermute | solution.py:265
  11.6 22.2 %collective-permute-start.2 = (bf16[512,128]{1,0:T(8,128)(2,1)}, bf16[512,128]{1,0:T(8,128)(2,1)}, u32[]{:S(2)}, u32[]{:S(2)}) collective-permute-start(bf16[512,128]{1,0:T(8,128)(2,1)} %param.23), channel_id=1, source_target_pairs={{0,1},{1,0},{2,3},{3,2},{4,5},{5,4},{6,7},{7,6},{8,9},{9,8},{10,11... | collective-permute-start | bytes 393224 | tf_op jit(solution)/shard_map/ppermute | solution.py:265
  11.6 82.2 %collective-permute-start.6 = (bf16[768,512]{1,0:T(8,128)(2,1)}, bf16[768,512]{1,0:T(8,128)(2,1)}, u32[]{:S(2)}, u32[]{:S(2)}) collective-permute-start(bf16[768,512]{1,0:T(8,128)(2,1)} %param.18), channel_id=1, source_target_pairs={{0,2},{2,0},{1,3},{3,1},{4,6},{6,4},{5,7},{7,5},{8,10},{10,8},{9,1... | collective-permute-start | bytes 2359304 | tf_op jit(solution)/shard_map/ppermute | solution.py:265
  16.0 75.3 %collective-permute-start.5 = (bf16[512,512]{1,0:T(8,128)(2,1)}, bf16[512,512]{1,0:T(8,128)(2,1)}, u32[]{:S(2)}, u32[]{:S(2)}) collective-permute-start(bf16[512,512]{1,0:T(8,128)(2,1)} %get-tuple-element.138), channel_id=1, source_target_pairs={{0,2},{2,0},{1,3},{3,1},{4,6},{6,4},{5,7},{7,5},{8,10},{10,8},{9,1... | collective-permute-start | bytes 1572872 | tf_op jit(solution)/shard_map/ppermute | solution.py:265
  28.3 47.0 %collective-permute-start.1 = (bf16[512,512]{1,0:T(8,128)(2,1)}, bf16[512,512]{1,0:T(8,128)(2,1)}, u32[]{:S(2)}, u32[]{:S(2)}) collective-permute-start(bf16[512,512]{1,0:T(8,128)(2,1)} %get-tuple-element.136), channel_id=1, source_target_pairs={{0,2},{2,0},{1,3},{3,1},{4,6},{6,4},{5,7},{7,5},{8,10},{10,8},{9,1... | collective-permute-start | bytes 1572872 | tf_op jit(solution)/shard_map/ppermute | solution.py:265
  33.8 61.9 %collective-permute-start.7 = (bf16[512,512]{1,0:T(8,128)(2,1)}, bf16[512,512]{1,0:T(8,128)(2,1)S(1)}, u32[]{:S(2)}, u32[]{:S(2)}) collective-permute-start(bf16[512,512]{1,0:T(8,128)(2,1)} %get-tuple-element.140), channel_id=1, source_target_pairs={{0,2},{2,0},{1,3},{3,1},{4,6},{6,4},{5,7},{7,5},{8,10},{10,8},{9,1... | collective-permute-start | bytes 1572872 | tf_op jit(solution)/shard_map/ppermute | solution.py:265
  35.1 36.4 %copy-start.47 = (bf16[512,128]{1,0:T(8,128)(2,1)}, bf16[512,128]{1,0:T(8,128)(2,1)S(1)}, u32[]{:S(2)}) copy-start(bf16[512,128]{1,0:T(8,128)(2,1)S(1)} %get-tuple-element.146) | copy-start | bytes 393220
  35.1 36.3 %collective-permute-start.3 = (bf16[512,256]{1,0:T(8,128)(2,1)S(1)}, bf16[512,256]{1,0:T(8,128)(2,1)S(1)}, u32[]{:S(2)}, u32[]{:S(2)}) collective-permute-start(bf16[512,256]{1,0:T(8,128)(2,1)S(1)} %pad_maximum_fusion.10), channel_id=1, source_target_pairs={{0,2},{2,0},{1,3},{3,1},{4,6},{6,4},{5,7},{7,5},{8,10},{10,8},{9,1... | collective-permute-start | bytes 786440 | tf_op jit(solution)/shard_map/ppermute | solution.py:265
  111.1 140.0 %reduce-scatter.3.cloned.1.call-start = ((), (), s32[]{:S(2)}) async-start(), calls=%async_computation.2 | async-start | bytes 3244032 | tf_op jit(solution)/shard_map/reduce_scatter | solution.py:364
  160.5 240.8 %all-gather.5.cloned.1.call-start = ((), (), s32[]{:S(2)}) async-start(), calls=%async_computation.5 | async-start | bytes 1179648 | tf_op jit(solution)/shard_map/all_gather | solution.py:346
  177.8 5.0 %collective-permute-start.14 = (bf16[64,512]{1,0:T(8,128)(2,1)}, bf16[64,512]{1,0:T(8,128)(2,1)}, u32[]{:S(2)}, u32[]{:S(2)}) collective-permute-start(bf16[64,512]{1,0:T(8,128)(2,1)} %get-tuple-element.149), channel_id=1, source_target_pairs={{0,2},{2,0},{1,3},{3,1},{4,6},{6,4},{5,7},{7,5},{8,10},{10,8},{9,1... | collective-permute-start | bytes 196616 | tf_op jit(solution)/shard_map/ppermute | solution.py:265
  182.7 81.4 %copy-start.39 = (bf16[768,8]{1,0:T(8,128)(2,1)S(1)}, bf16[768,8]{1,0:T(8,128)(2,1)}, u32[]{:S(2)}) copy-start(bf16[768,8]{1,0:T(8,128)(2,1)} %copy-done.38) | copy-start | bytes 36868
  182.7 81.4 %copy-start.74 = (bf16[512,8]{0,1:T(8,128)(2,1)S(1)}, bf16[512,8]{0,1:T(8,128)(2,1)}, u32[]{:S(2)}) copy-start(bf16[512,8]{0,1:T(8,128)(2,1)} %get-tuple-element.150) | copy-start | bytes 24580
  252.0 5.6 %collective-permute-start.12 = (bf16[64,1408]{1,0:T(8,128)(2,1)S(1)}, bf16[64,1408]{1,0:T(8,128)(2,1)S(1)}, u32[]{:S(2)}, u32[]{:S(2)}) collective-permute-start(bf16[64,1408]{1,0:T(8,128)(2,1)S(1)} %slice.230), channel_id=1, source_target_pairs={{0,2},{2,0},{1,3},{3,1},{4,6},{6,4},{5,7},{7,5},{8,10},{10,8},{9,1... | collective-permute-start | bytes 540680 | tf_op jit(solution)/shard_map/ppermute | solution.py:265
  254.2 150.0 %all-gather.3.cloned.1.call-start = ((), (), s32[]{:S(2)}) async-start(), calls=%async_computation.3 | async-start | bytes 2801664 | tf_op jit(solution)/shard_map/all_gather | solution.py:381
  258.4 3.6 collective-permute-start.13
  270.8 20.5 %collective-permute-start.10 = (bf16[768,512]{1,0:T(8,128)(2,1)S(1)}, bf16[768,512]{1,0:T(8,128)(2,1)S(1)}, u32[]{:S(2)}, u32[]{:S(2)}) collective-permute-start(bf16[768,512]{1,0:T(8,128)(2,1)S(1)} %slice.276), channel_id=1, source_target_pairs={{0,2},{2,0},{1,3},{3,1},{4,6},{6,4},{5,7},{7,5},{8,10},{10,8},{9,1... | collective-permute-start | bytes 2359304 | tf_op jit(solution)/shard_map/ppermute | solution.py:265
  273.6 34.1 %collective-permute-start.8 = (bf16[768,512]{1,0:T(8,128)(2,1)S(1)}, bf16[768,512]{1,0:T(8,128)(2,1)S(1)}, u32[]{:S(2)}, u32[]{:S(2)}) collective-permute-start(bf16[768,512]{1,0:T(8,128)(2,1)S(1)} %slice.277), channel_id=1, source_target_pairs={{0,2},{2,0},{1,3},{3,1},{4,6},{6,4},{5,7},{7,5},{8,10},{10,8},{9,1... | collective-permute-start | bytes 2359304 | tf_op jit(solution)/shard_map/ppermute | solution.py:265
  292.4 59.4 %copy-start.98 = (f32[512]{0:T(512)S(1)}, f32[512]{0:T(512)}, u32[]{:S(2)}) copy-start(f32[512]{0:T(512)} %get-tuple-element.104) | copy-start | bytes 6148
  292.4 60.7 %collective-permute-start.11 = (bf16[768,256]{1,0:T(8,128)(2,1)}, bf16[768,256]{1,0:T(8,128)(2,1)S(1)}, u32[]{:S(2)}, u32[]{:S(2)}) collective-permute-start(bf16[768,256]{1,0:T(8,128)(2,1)} %dynamic-slice_convert_fusion), channel_id=1, source_target_pairs={{0,1},{1,0},{2,3},{3,2},{4,5},{5,4},{6,7},{7,6},{8,9},{9,8},{10,11... | collective-permute-start | bytes 1179656 | tf_op jit(solution)/shard_map/ppermute | solution.py:265
  309.9 87.9 %collective-permute-start.9 = (bf16[768,256]{1,0:T(8,128)(2,1)}, bf16[768,256]{1,0:T(8,128)(2,1)}, u32[]{:S(2)}, u32[]{:S(2)}) collective-permute-start(bf16[768,256]{1,0:T(8,128)(2,1)} %dynamic-slice_convert_fusion.1), channel_id=1, source_target_pairs={{0,1},{1,0},{2,3},{3,2},{4,5},{5,4},{6,7},{7,6},{8,9},{9,8},{10,11... | collective-permute-start | bytes 1179656 | tf_op jit(solution)/shard_map/ppermute | solution.py:265
  354.6 45.7 %copy-start.72 = (f32[768]{0:T(1024)S(1)}, f32[768]{0:T(1024)}, u32[]{:S(2)}) copy-start(f32[768]{0:T(1024)} %add_rsqrt_fusion) | copy-start | bytes 9220
  (110 other events, 779.2 us)
Sparse Core Ops, SparseCore 0:
  111.2 65.0 reduce-scatter.4
  179.8 71.2 reduce-scatter.2
  254.3 38.5 all-gather.4
  295.0 51.9 all-gather.2

commit v2 on v1

--- a/solution.py
+++ b/solution.py
@@ -294,10 +294,13 @@
         return jnp.concatenate([mine, theirs], axis=1 - axis)
 
     wx = own_heads(w_x, 1)
-    wbc_cols = ordered(w_bc, swap(w_bc, "col"), col, 1)
-    wbc = jnp.concatenate([wbc_cols, swap(wbc_cols, "row")], axis=0)
+    wbc_rows = jnp.concatenate([w_bc, swap(w_bc, "row")], axis=0)
+    wbc = ordered(wbc_rows, swap(wbc_rows, "col"), col, 1)
     wdt = own_heads(w_dt, 1)
     gain = jnp.concatenate([rmsnorm_gain, swap(rmsnorm_gain, "row")])
+    wx, wbc_rows, w_z, w_out, out_grad = lax.optimization_barrier(
+        (wx, wbc_rows, w_z, w_out, out_grad)
+    )
     wz = own_heads(w_z, 1)
     incoming = jnp.concatenate([out_grad, swap(out_grad, "row")], axis=1)
     wo = own_heads(w_out, 0)
@@ -362,6 +365,36 @@
     wide = big.shape[1]
     big = big.reshape(2, batches, -1, wide).transpose(1, 0, 2, 3).reshape(-1, wide)
     piece = lax.psum_scatter(big, "dp", scatter_dimension=0, tiled=True)
+    back = dot(dz, wz.T) + dot(dx, wx.T) + dot(ddt, wdt.T) + dot(dbc, wbc.T)
+    d_normed = scattered(back)
+    xhat_own = part(xhat[:, :half], col, 1)
+    scaled = d_normed * part(rmsnorm_gain, col, 0)[None, :]
+    total = lax.psum(jnp.sum(scaled * xhat_own, axis=1), ("row", "col"))
+    hidden_input_gradient = (
+        part(out_grad, col, 1).astype(F32)
+        + scale[:, None] * (scaled - xhat_own * (total / model_width)[:, None])
+    ).astype(BF16)
+    norm_gradient = jnp.sum(d_normed * xhat_own, axis=0)
+
+    small = (grad_bw, grad_bb, norm_gradient, grad_cw, grad_cb, grad_shift, grad_alog, grad_skip,
+             grad_gate)
+    shared = jnp.concatenate([grad_bw.reshape(-1), grad_bb])
+    shared = shared + swap(shared, "row")
+    shared = shared + swap(shared, "col")
+    packed = jnp.concatenate([shared] + [v.reshape(-1) for v in small[2:]])
+    distance = 1
+    while distance < batches:
+        packed = packed + lax.ppermute(packed, "dp", [(i, i ^ distance) for i in range(batches)])
+        distance *= 2
+    sums, start = [], 0
+    for v in small:
+        sums.append(packed[start : start + v.size].reshape(v.shape))
+        start += v.size
+    (grad_bw, grad_bb, norm_gradient, grad_cw, grad_cb, grad_shift, grad_alog, grad_skip,
+     grad_gate) = sums
+    piece, packed, hidden_input_gradient = lax.optimization_barrier(
+        (piece, packed, hidden_input_gradient)
+    )
     piece = piece.reshape(2, -1, wide)
     mine, theirs = piece[0], swap(piece[1], "row")
     nz, nbc = dz.shape[1], dbc.shape[1]
@@ -388,21 +421,6 @@
         [whole_grads[:, at : at + steps], whole_grads[:, at + LANES : at + LANES + steps]], axis=1
     ).astype(F32)
 
-    back = dot(dz, wz.T) + dot(dx, wx.T) + dot(ddt, wdt.T) + dot(dbc, wbc.T)
-    d_normed = scattered(back)
-    xhat_own = part(xhat[:, :half], col, 1)
-    scaled = d_normed * part(rmsnorm_gain, col, 0)[None, :]
-    total = lax.psum(jnp.sum(scaled * xhat_own, axis=1), ("row", "col"))
-    hidden_input_gradient = (
-        part(out_grad, col, 1).astype(F32)
-        + scale[:, None] * (scaled - xhat_own * (total / model_width)[:, None])
-    ).astype(BF16)
-    norm_gradient = jnp.sum(d_normed * xhat_own, axis=0)
-
-    (norm_gradient, grad_cw, grad_cb, grad_shift, grad_alog, grad_skip, grad_gate) = lax.psum(
-        (norm_gradient, grad_cw, grad_cb, grad_shift, grad_alog, grad_skip, grad_gate), "dp"
-    )
-    grad_bw, grad_bb = lax.psum((grad_bw, grad_bb), ("dp", "row", "col"))
     return (
         block_out,
         hidden_input_gradient,

time: 424 us -> 356 us (0.84)
  blocking collectives: 91.7 us -> 13.9 us
  starting transfers between devices: 15.5 us -> 21.2 us
  other arithmetic: 50 us -> 55.5 us
  matrix products: 28.1 us -> 22.7 us
    psum x2 -> x0, blocking collectives: 79.2 us -> none  [the longest x1 41.9 us: per_device(): grad_bw, grad_bb = lax.psum((grad_bw, grad_bb), ('dp', 'row', 'col'))]
    all_gather x1, waiting for transfers between devices: 0.01 us -> 51.5 us  [per_device(): whole_grads = lax.all_gather(pieces, 'dp', axis=0, tiled=True)]
    reduce_scatter x1, waiting for transfers between devices: 67.4 us -> 32.5 us  [per_device(): piece = lax.psum_scatter(big, 'dp', scatter_dimension=0, tiled=True)]
    reduce_scatter x1, waiting for transfers between devices: 15.7 us -> 0.01 us  [per_device(): wo_piece = lax.psum_scatter(grad_wo, 'dp', scatter_dimension=0, tiled=True)]
    dot_general x12, matrix products: 28.1 us -> 22.7 us  [dot(): return jnp.dot(a, b, preferred_element_type=F32)]
    ppermute x0 -> x3, starting transfers between devices: none -> 4.97 us  [per_device(): lax.ppermute(packed, 'dp', [(i, i ^ distance) for i in range(batches)])]
    ppermute x15 -> x17, waiting for transfers between devices: 64.7 us -> 60.3 us  [swap(): lax.ppermute(value, axis, [(i, (i + 1) % count) for i in range(count)])]
    ppermute x15 -> x17, starting transfers between devices: 15.1 us -> 16.1 us  [swap(): lax.ppermute(value, axis, [(i, (i + 1) % count) for i in range(count)])]
  transfers between devices with their start and end apart: 19 -> 24, of which waited for: 6 -> 11; matrix products, arithmetic and copies ran while one was open for 21% -> 26% of each run, Pallas kernels for 8% -> 9%
where the time goes in v2:
time: 356 us; the launch traced here: 350 us
  waiting for transfers between devices  149 us (42%)
  other arithmetic  55.5 us (16%)
  local copies, waits for them, and re-layouts  39.2 us (11%)
  Pallas kernels  33.1 us (9%)
  matrix products  22.7 us (6%)
  starting transfers between devices  21.2 us (6%)
  between operations  15.4 us (4%)
  blocking collectives  13.9 us (4%)
    ppermute x17, waiting for transfers between devices, swap(): lax.ppermute(value, axis, [(i, (i + 1) % count) for i in range(count)])  60.3 us
    all_gather x1, waiting for transfers between devices, per_device(): whole_grads = lax.all_gather(pieces, 'dp', axis=0, tiled=True)  51.5 us
    reduce_scatter x1, waiting for transfers between devices, per_device(): piece = lax.psum_scatter(big, 'dp', scatter_dimension=0, tiled=True)  32.5 us
    pallas_call x1, Pallas kernels, mixer(): state_scan(x_act, bc_act[:, :state], bc_act[:, state:], steps, jnp.exp(a_...  22.9 us
    dot_general x12, matrix products, dot(): return jnp.dot(a, b, preferred_element_type=F32)  22.7 us
    ppermute x17, starting transfers between devices, swap(): lax.ppermute(value, axis, [(i, (i + 1) % count) for i in range(count)])  16.1 us
    pallas_call x1, Pallas kernels, scan_fwd(): pl.pallas_call(scan_forward, grid=(count,), in_specs=ins, out_specs=[tall...  10.2 us
    unnamed x228, local copies, waits for them, and re-layouts  9.83 us
  transfers between devices with their start and end apart: 24, of which 11 were waited for; matrix products, arithmetic and copies ran while one was open for 26% of the time, Pallas kernels for 9%

profile of v2, /device:TPU:0, one launch (start us, length us, event | category | flops | bytes accessed | tf_op | source)
XLA Modules:
  0.0 349.7 jit_solution(2052591000147952560)
XLA Ops:
  7.3 3.0 collective-permute-start
  13.7 2.2 constant_dynamic-slice_fusion.7
  26.3 2.8 multiply_convert_fusion
  45.8 2.2 fusion.6
  48.1 10.2 %jvp_scan_forward_.1 = (f32[768,512]{1,0:T(8,128)S(1)}, f32[3,128,512]{2,1,0:T(8,128)S(1)}) custom-call(f32[768,512]{1,0:T(8,128)S(1)} %get-tuple-element.121.x_ref, f32[768,128]{1,0:T(8,128)S(1)} %get-tuple-element.148.b_ref, f32[768,128]{1,0:T(8,128)S(1)} %get-tuple-element.147.c_ref, f32[768,8]{1,0:T(8,128)S(1)} %copy-done.10, f32[8,768]{1,0:T(8,128)S(1)} %copy-done.8, ...), custom_call_target="tpu_custom_call" | custom-call | flops 2000000000 | bytes 6000000 | tf_op jit(solution)/shard_map/jvp(scan_forward)/pallas_call | solution.py:201
  58.5 13.6 %collective-permute-done.5 = bf16[512,512]{1,0:T(8,128)(2,1)S(1)} collective-permute-done((bf16[512,512]{1,0:T(8,128)(2,1)S(1)}, bf16[512,512]{1,0:T(8,128)(2,1)S(1)}, u32[]{:S(2)}, u32[]{:S(2)}) %collective-permute-start.5) | collective-permute-done | bytes 524320 | tf_op jit(solution)/shard_map/ppermute | solution.py:265
  73.3 9.7 %collective-permute-done.7 = bf16[512,512]{1,0:T(8,128)(2,1)S(1)} collective-permute-done((bf16[512,512]{1,0:T(8,128)(2,1)S(1)}, bf16[512,512]{1,0:T(8,128)(2,1)S(1)}, u32[]{:S(2)}, u32[]{:S(2)}) %collective-permute-start.7) | collective-permute-done | bytes 524320 | tf_op jit(solution)/shard_map/ppermute | solution.py:265
  83.0 3.2 multiply_reduce_fusion.8
  86.3 6.7 %psum.14 = f32[2,768]{1,0:T(2,128)S(1)} all-reduce(f32[2,768]{1,0:T(2,128)S(1)} %pad_maximum_fusion.17), channel_id=1, replica_groups=mesh['dp'=8,'row'=2,'col'=2] {'row','col'}, use_global_device_ids=true, to_apply=%region_5.6 | all-reduce | flops 1536 | bytes 12288 | tf_op jit(solution)/shard_map/psum | solution.py:332
  94.3 4.1 %convolution_convert_fusion.1 = bf16[512,1024]{1,0:T(8,128)(2,1)} fusion(bf16[768,1024]{1,0:T(8,128)(2,1)} %copy-done.55, f32[768,512]{1,0:T(8,128)} %get-tuple-element.118, f32[768]{0:T(1024)S(1)} %get-tuple-element.99, f32[512]{0:T(512)} %bitcast.123), kind=kOutput, calls=%fused_computation.38 | convolution fusion | flops 807010304 | bytes 4199424 | tf_op jit(solution)/shard_map/dot_general | solution.py:279
  98.5 5.6 %multiply_reduce_fusion.2 = (f32[512]{0:T(512)}, f32[768,512]{1,0:T(8,128)}, bf16[768,512]{1,0:T(8,128)(2,1)}, f32[512]{0:T(512)}) fusion(f32[768,512]{1,0:T(8,128)S(1)} %copy-done.23, f32[768,512]{1,0:T(8,128)} %copy-done.44, f32[768]{0:T(1024)} %get-tuple-element.171, f32[768]{0:T(1024)} %get-tuple-element.98, f32[768,512]{1,0:T(8,128)} %get-tuple-element.118, ...), kind=kLoop, calls=%fused_computation.20 | loop fusion | flops 11795456 | bytes 10244096 | tf_op jit(solution)/shard_map/transpose(jvp())/reduce_sum | solution.py:259
  104.2 22.9 %transpose_jvp_scan_backward__.1 = (f32[768,512]{1,0:T(8,128)S(1)}, f32[768,128]{1,0:T(8,128)S(1)}, f32[768,128]{1,0:T(8,128)S(1)}, f32[768,8]{1,0:T(8,128)S(1)}, f32[1,8]{1,0:T(1,128)S(1)}) custom-call(f32[768,512]{1,0:T(8,128)} %copy-done, f32[768,128]{1,0:T(8,128)S(1)} %copy-done.7, f32[768,128]{1,0:T(8,128)S(1)} %copy-done.5, f32[768,8]{1,0:T(8,128)S(1)} %copy-done.11, ...), custom_call_target="tpu_custom_call" | custom-call | flops 6000000000 | bytes 10000000 | tf_op jit(solution)/shard_map/transpose(jvp(scan_backward))/pallas_call | solution.py:256
  138.7 3.0 concatenate.99
  141.7 4.8 %convolution_convert_fusion = bf16[1024,1408]{1,0:T(8,128)(2,1)S(1)} fusion(bf16[768,1024]{1,0:T(8,128)(2,1)} %copy-done.42, bf16[768,1408]{1,0:T(8,128)(2,1)} %concatenate.99), kind=kOutput, calls=%fused_computation | convolution fusion | flops 2216034304 | bytes 6619136 | tf_op jit(solution)/shard_map/dot_general | solution.py:279
  155.8 2.7 slice.264
  159.9 13.2 %collective-permute-done.12 = bf16[768,512]{1,0:T(8,128)(2,1)} collective-permute-done((bf16[768,512]{1,0:T(8,128)(2,1)}, bf16[768,512]{1,0:T(8,128)(2,1)}, u32[]{:S(2)}, u32[]{:S(2)}) %collective-permute-start.12) | collective-permute-done | bytes 786464 | tf_op jit(solution)/shard_map/ppermute | solution.py:265
  185.8 7.1 %psum.15 = f32[768]{0:T(1024)S(1)} all-reduce(f32[768]{0:T(1024)S(1)} %get-tuple-element.90), channel_id=1, replica_groups=mesh['dp'=8,'row'=2,'col'=2] {'row','col'}, use_global_device_ids=true, to_apply=%region_23.24 | all-reduce | flops 768 | bytes 6144 | tf_op jit(solution)/shard_map/psum | solution.py:372
  195.3 3.4 collective-permute-done.15
  206.2 32.5 %reduce-scatter.3.cloned.1.call-done = bf16[128,1408]{1,0:T(8,128)(2,1)} async-done(((bf16[1024,1408]{1,0:T(8,128)(2,1)}), bf16[128,1408]{1,0:T(8,128)(2,1)}) %reduce-scatter.3.cloned.1.call-update) | async-done | bytes 360464 | tf_op jit(solution)/shard_map/reduce_scatter | solution.py:367
  242.0 3.3 collective-permute-done.17
  255.6 18.5 %collective-permute-done.8 = bf16[768,512]{1,0:T(8,128)(2,1)S(1)} collective-permute-done((bf16[768,512]{1,0:T(8,128)(2,1)S(1)}, bf16[768,512]{1,0:T(8,128)(2,1)S(1)}, u32[]{:S(2)}, u32[]{:S(2)}) %collective-permute-start.8) | collective-permute-done | bytes 786464 | tf_op jit(solution)/shard_map/ppermute | solution.py:265
  281.1 2.8 bitcast_convert_fusion
  283.9 51.5 %all-gather.3.cloned.1.call-done = bf16[512,2432]{1,0:T(8,128)(2,1)} async-done(((bf16[64,2432]{1,0:T(8,128)(2,1)}), bf16[512,2432]{1,0:T(8,128)(2,1)}) %all-gather.3.cloned.1.call-update) | async-done | bytes 2490384 | tf_op jit(solution)/shard_map/all_gather | solution.py:414
  338.8 4.0 %slice_convert_fusion.2 = (f32[512,1024]{1,0:T(8,128)}, f32[512,1024]{1,0:T(8,128)}) fusion(bf16[512,2432]{1,0:T(8,128)(2,1)} %all-gather.3.cloned.1.call-done), kind=kLoop, calls=%fused_computation.45 | loop fusion | flops 1048576 | bytes 6291456 | tf_op jit(solution)/shard_map/convert_element_type | solution.py:416
  (384 shorter events, 101.1 us)
Async XLA Ops:
  7.2 193.8 %reduce-scatter.5.cloned.1.call-start = ((), (), s32[]{:S(2)}) async-start(), calls=%async_computation.4 | async-start | bytes 1179648 | tf_op jit(solution)/shard_map/reduce_scatter | solution.py:346
  7.3 18.3 %collective-permute-start = (f32[512]{0:T(512)}, f32[512]{0:T(512)}, u32[]{:S(2)}, u32[]{:S(2)}) collective-permute-start(f32[512]{0:T(512)} %param.20), channel_id=1, source_target_pairs={{0,2},{2,0},{1,3},{3,1},{4,6},{6,4},{5,7},{7,5},{8,10},{10,8},{9,1... | collective-permute-start | bytes 6152 | tf_op jit(solution)/shard_map/ppermute | solution.py:265
  11.6 19.2 %collective-permute-start.4 = (bf16[512,8]{0,1:T(8,128)(2,1)}, bf16[512,8]{0,1:T(8,128)(2,1)}, u32[]{:S(2)}, u32[]{:S(2)}) collective-permute-start(bf16[512,8]{0,1:T(8,128)(2,1)} %get-tuple-element.161), channel_id=1, source_target_pairs={{0,2},{2,0},{1,3},{3,1},{4,6},{6,4},{5,7},{7,5},{8,10},{10,8},{9,1... | collective-permute-start | bytes 24584 | tf_op jit(solution)/shard_map/ppermute | solution.py:265
  11.8 17.3 %collective-permute-start.2 = (bf16[512,128]{1,0:T(8,128)(2,1)}, bf16[512,128]{1,0:T(8,128)(2,1)}, u32[]{:S(2)}, u32[]{:S(2)}) collective-permute-start(bf16[512,128]{1,0:T(8,128)(2,1)} %param.23), channel_id=1, source_target_pairs={{0,2},{2,0},{1,3},{3,1},{4,6},{6,4},{5,7},{7,5},{8,10},{10,8},{9,1... | collective-permute-start | bytes 393224 | tf_op jit(solution)/shard_map/ppermute | solution.py:265
  15.9 22.2 %collective-permute-start.1 = (bf16[512,512]{1,0:T(8,128)(2,1)}, bf16[512,512]{1,0:T(8,128)(2,1)}, u32[]{:S(2)}, u32[]{:S(2)}) collective-permute-start(bf16[512,512]{1,0:T(8,128)(2,1)} %get-tuple-element.143), channel_id=1, source_target_pairs={{0,2},{2,0},{1,3},{3,1},{4,6},{6,4},{5,7},{7,5},{8,10},{10,8},{9,1... | collective-permute-start | bytes 1572872 | tf_op jit(solution)/shard_map/ppermute | solution.py:265
  30.8 3.8 %collective-permute-start.3 = (bf16[1024,128]{1,0:T(8,128)(2,1)}, bf16[1024,128]{1,0:T(8,128)(2,1)S(1)}, u32[]{:S(2)}, u32[]{:S(2)}) collective-permute-start(bf16[1024,128]{1,0:T(8,128)(2,1)} %constant_dynamic-update-slice_fusion), channel_id=1, source_target_pairs={{0,1},{1,0},{2,3},{3,2},{4,5},{5,4},{6,7},{7,6},{8,9},{9,8},{10,11... | collective-permute-start | bytes 786440 | tf_op jit(solution)/shard_map/ppermute | solution.py:265
  40.4 32.8 %collective-permute-start.6 = (bf16[768,512]{1,0:T(8,128)(2,1)S(1)}, bf16[768,512]{1,0:T(8,128)(2,1)S(1)}, u32[]{:S(2)}, u32[]{:S(2)}) collective-permute-start(bf16[768,512]{1,0:T(8,128)(2,1)S(1)} %copy-done.39), channel_id=1, source_target_pairs={{0,2},{2,0},{1,3},{3,1},{4,6},{6,4},{5,7},{7,5},{8,10},{10,8},{9,1... | collective-permute-start | bytes 2359304 | tf_op jit(solution)/shard_map/ppermute | solution.py:265
  42.4 29.7 %collective-permute-start.5 = (bf16[512,512]{1,0:T(8,128)(2,1)S(1)}, bf16[512,512]{1,0:T(8,128)(2,1)S(1)}, u32[]{:S(2)}, u32[]{:S(2)}) collective-permute-start(bf16[512,512]{1,0:T(8,128)(2,1)S(1)} %get-tuple-element.139), channel_id=1, source_target_pairs={{0,2},{2,0},{1,3},{3,1},{4,6},{6,4},{5,7},{7,5},{8,10},{10,8},{9,1... | collective-permute-start | bytes 1572872 | tf_op jit(solution)/shard_map/ppermute | solution.py:265
  42.8 40.2 %collective-permute-start.7 = (bf16[512,512]{1,0:T(8,128)(2,1)S(1)}, bf16[512,512]{1,0:T(8,128)(2,1)S(1)}, u32[]{:S(2)}, u32[]{:S(2)}) collective-permute-start(bf16[512,512]{1,0:T(8,128)(2,1)S(1)} %get-tuple-element.141), channel_id=1, source_target_pairs={{0,2},{2,0},{1,3},{3,1},{4,6},{6,4},{5,7},{7,5},{8,10},{10,8},{9,1... | collective-permute-start | bytes 1572872 | tf_op jit(solution)/shard_map/ppermute | solution.py:265
  98.4 140.4 %reduce-scatter.3.cloned.1.call-start = ((), (), s32[]{:S(2)}) async-start(), calls=%async_computation.2 | async-start | bytes 3244032 | tf_op jit(solution)/shard_map/reduce_scatter | solution.py:367
  148.4 132.7 %all-gather.5.cloned.1.call-start = ((), (), s32[]{:S(2)}) async-start(), calls=%async_computation.5 | async-start | bytes 1179648 | tf_op jit(solution)/shard_map/all_gather | solution.py:349
  154.3 18.8 %collective-permute-start.12 = (bf16[768,512]{1,0:T(8,128)(2,1)}, bf16[768,512]{1,0:T(8,128)(2,1)}, u32[]{:S(2)}, u32[]{:S(2)}) collective-permute-start(bf16[768,512]{1,0:T(8,128)(2,1)} %slice.319), channel_id=1, source_target_pairs={{0,2},{2,0},{1,3},{3,1},{4,6},{6,4},{5,7},{7,5},{8,10},{10,8},{9,1... | collective-permute-start | bytes 2359304 | tf_op jit(solution)/shard_map/ppermute | solution.py:265
  158.7 17.2 %collective-permute-start.10 = (f32[1280]{0:T(1024)S(1)}, f32[1280]{0:T(1024)S(1)}, u32[]{:S(2)}, u32[]{:S(2)}) collective-permute-start(f32[1280]{0:T(1024)S(1)} %pad_maximum_fusion.16), channel_id=1, source_target_pairs={{0,2},{2,0},{1,3},{3,1},{4,6},{6,4},{5,7},{7,5},{8,10},{10,8},{9,1... | collective-permute-start | bytes 15368 | tf_op jit(solution)/shard_map/ppermute | solution.py:265
  175.3 5.7 %collective-permute-start.13 = (bf16[768,256]{1,0:T(8,128)(2,1)}, bf16[768,256]{1,0:T(8,128)(2,1)S(1)}, u32[]{:S(2)}, u32[]{:S(2)}) collective-permute-start(bf16[768,256]{1,0:T(8,128)(2,1)} %dynamic-slice_convert_fusion), channel_id=1, source_target_pairs={{0,1},{1,0},{2,3},{3,2},{4,5},{5,4},{6,7},{7,6},{8,9},{9,8},{10,11... | collective-permute-start | bytes 1179656 | tf_op jit(solution)/shard_map/ppermute | solution.py:265
  175.9 3.9 %collective-permute-start.11 = (f32[1280]{0:T(1024)S(1)}, f32[1280]{0:T(1024)}, u32[]{:S(2)}, u32[]{:S(2)}) collective-permute-start(f32[1280]{0:T(1024)S(1)} %fusion.32), channel_id=1, source_target_pairs={{0,1},{1,0},{2,3},{3,2},{4,5},{5,4},{6,7},{7,6},{8,9},{9,8},{10,11... | collective-permute-start | bytes 15368 | tf_op jit(solution)/shard_map/ppermute | solution.py:265
  184.2 8.8 %collective-permute-start.14 = (f32[4632]{0:T(1024)}, f32[4632]{0:T(1024)}, u32[]{:S(2)}, u32[]{:S(2)}) collective-permute-start(f32[4632]{0:T(1024)} %concatenate.101), channel_id=1, source_target_pairs={{0,4},{4,0},{8,12},{12,8},{16,20},{20,16},{24,28},{28,24},{1,5},{5... | collective-permute-start | bytes 55592 | tf_op jit(solution)/shard_map/ppermute | solution.py:387
  193.7 5.0 %collective-permute-start.15 = (f32[4632]{0:T(1024)S(1)}, f32[4632]{0:T(1024)S(1)}, u32[]{:S(2)}, u32[]{:S(2)}) collective-permute-start(f32[4632]{0:T(1024)S(1)} %add.266), channel_id=1, source_target_pairs={{0,8},{4,12},{8,0},{12,4},{16,24},{20,28},{24,16},{28,20},{1,9},{5... | collective-permute-start | bytes 55592 | tf_op jit(solution)/shard_map/ppermute | solution.py:387
  199.3 5.6 %collective-permute-start.16 = (f32[4632]{0:T(1024)}, f32[4632]{0:T(1024)}, u32[]{:S(2)}, u32[]{:S(2)}) collective-permute-start(f32[4632]{0:T(1024)} %add.267), channel_id=1, source_target_pairs={{0,16},{4,20},{8,24},{12,28},{16,0},{20,4},{24,8},{28,12},{1,17},{... | collective-permute-start | bytes 55592 | tf_op jit(solution)/shard_map/ppermute | solution.py:387
  201.9 4.3 %collective-permute-start.19 = (bf16[64,512]{1,0:T(8,128)(2,1)S(1)}, bf16[64,512]{1,0:T(8,128)(2,1)S(1)}, u32[]{:S(2)}, u32[]{:S(2)}) collective-permute-start(bf16[64,512]{1,0:T(8,128)(2,1)S(1)} %get-tuple-element.152), channel_id=1, source_target_pairs={{0,2},{2,0},{1,3},{3,1},{4,6},{6,4},{5,7},{7,5},{8,10},{10,8},{9,1... | collective-permute-start | bytes 196616 | tf_op jit(solution)/shard_map/ppermute | solution.py:265
  239.7 5.6 %collective-permute-start.17 = (bf16[64,1408]{1,0:T(8,128)(2,1)S(1)}, bf16[64,1408]{1,0:T(8,128)(2,1)S(1)}, u32[]{:S(2)}, u32[]{:S(2)}) collective-permute-start(bf16[64,1408]{1,0:T(8,128)(2,1)S(1)} %slice.222), channel_id=1, source_target_pairs={{0,2},{2,0},{1,3},{3,1},{4,6},{6,4},{5,7},{7,5},{8,10},{10,8},{9,1... | collective-permute-start | bytes 540680 | tf_op jit(solution)/shard_map/ppermute | solution.py:265
  241.9 93.5 %all-gather.3.cloned.1.call-start = ((), (), s32[]{:S(2)}) async-start(), calls=%async_computation.3 | async-start | bytes 2801664 | tf_op jit(solution)/shard_map/all_gather | solution.py:414
  246.1 3.5 %collective-permute-start.18 = (bf16[64,128]{1,0:T(8,128)(2,1)S(1)}, bf16[64,128]{1,0:T(8,128)(2,1)S(1)}, u32[]{:S(2)}, u32[]{:S(2)}) collective-permute-start(bf16[64,128]{1,0:T(8,128)(2,1)S(1)} %dynamic-slice_convert_fusion.2), channel_id=1, source_target_pairs={{0,1},{1,0},{2,3},{3,2},{4,5},{5,4},{6,7},{7,6},{8,9},{9,8},{10,11... | collective-permute-start | bytes 49160 | tf_op jit(solution)/shard_map/ppermute | solution.py:265
  254.1 20.0 %collective-permute-start.8 = (bf16[768,512]{1,0:T(8,128)(2,1)S(1)}, bf16[768,512]{1,0:T(8,128)(2,1)S(1)}, u32[]{:S(2)}, u32[]{:S(2)}) collective-permute-start(bf16[768,512]{1,0:T(8,128)(2,1)S(1)} %slice.320), channel_id=1, source_target_pairs={{0,2},{2,0},{1,3},{3,1},{4,6},{6,4},{5,7},{7,5},{8,10},{10,8},{9,1... | collective-permute-start | bytes 2359304 | tf_op jit(solution)/shard_map/ppermute | solution.py:265
  274.5 1.8 collective-permute-start.9
  (110 other events, 1066.7 us)
Sparse Core Ops, SparseCore 0:
  98.5 64.9 reduce-scatter.4
  167.0 71.6 reduce-scatter.2
  242.1 38.9 all-gather.4
  283.7 51.7 all-gather.2
